TPU v7x, 32 devices: a whole 2x2x4 slice. The times are simulated.
32 devices in a mesh: gx: 4 (over y, x), gy: 4 (over z), ga: 2 (over core).
Axes of the slice: x: 2, y: 2, z: 4, core: 2. Of those that a mesh axis runs over, the one named last changes fastest.
Arguments:
- fields: float32 [5, 16, 64, 1024], P(None, 'ga', 'gx', 'gy'), may hold values from -6 to 6
- stiffness: float32 [16, 64, 1024], P('ga', 'gx', 'gy'), may hold values from 0.25 to 4
- lift_weight: float32 [5, 32], replicated, may hold values from -2.5 to 2.5
- lift_bias: float32 [32], replicated, may hold values from -3 to 3
- mix_weight: bfloat16 [32, 32], replicated, may hold values from -0.5 to 0.5
- spectral_weight: float32 [8, 32, 32, 32, 128], P('ga', 'gy', None, 'gx'), may hold values from -0.48 to 0.48
- output_bias: float32 [32], replicated, may hold values from -3 to 3
Outputs:
- layer_out: bfloat16 [16, 32, 32, 512], P('ga', None, 'gx', 'gy')
All inputs are finite; a program needn't handle non-finite values.
Results may differ from a plain program's by a relative error of at most 0.01.
Values may be sent and summed in bfloat16 or wider, within the bound.
A program may use at most 128 MiB of HBM per device.

v0:
```python
import math

import jax
import jax.numpy as jnp
from jax import lax
from jax.sharding import PartitionSpec as P

STEPS = 3
MX = 32
MY = 64
MZ = 8


courant_half = 0.1
smooth_half = 0.15
mean_flow = (0.3, -0.2, 0.1)
highest = lax.Precision.HIGHEST


def padded_2(block, sides, width):
    for axis, dim in sides:
        count = lax.axis_size(axis)
        forward = [(i, i + 1) for i in range(count - 1)]
        forward.append((count - 1, 0))
        backward = [(target, source) for source, target in forward]
        low = lax.ppermute(
            lax.slice_in_dim(block, block.shape[dim] - width, None, axis=dim), axis, forward
        )
        high = lax.ppermute(lax.slice_in_dim(block, 0, width, axis=dim), axis, backward)
        block = jnp.concatenate([low, block, high], axis=dim)
    return block


def step_interior(padded, stiff_part):
    center = padded[:, 1:-1, 1:-1, 1:-1]
    upper_depth = padded[:, 2:, 1:-1, 1:-1]
    lower_depth = padded[:, :-2, 1:-1, 1:-1]
    upper_east = padded[:, 1:-1, 2:, 1:-1]
    lower_east = padded[:, 1:-1, :-2, 1:-1]
    upper_north = padded[:, 1:-1, 1:-1, 2:]
    lower_north = padded[:, 1:-1, 1:-1, :-2]
    slope_depth = upper_depth - lower_depth
    slope_east = upper_east - lower_east
    slope_north = upper_north - lower_north
    curvature = (
        upper_depth
        + lower_depth
        + upper_east
        + lower_east
        + upper_north
        + lower_north
        - 6.0 * center
    )
    transport = mean_flow[0] * slope_east + mean_flow[1] * slope_north + mean_flow[2] * slope_depth
    diverge = slope_east[1] + slope_north[2] + slope_depth[3]
    coupling = jnp.stack(
        [diverge, slope_east[4], slope_north[4], slope_depth[4], stiff_part * diverge]
    )
    return center - courant_half * (transport + coupling) + smooth_half * curvature


def trim(block, margin):
    return block[margin:-margin, margin:-margin, margin:-margin]


def coarsen(fields_now):
    extent = fields_now.shape
    blocks = fields_now.reshape(extent[0], extent[1], extent[2] // 2, 2, extent[3] // 2, 2)
    return 0.25 * (
        blocks[:, :, :, 0, :, 0]
        + blocks[:, :, :, 1, :, 0]
        + blocks[:, :, :, 0, :, 1]
        + blocks[:, :, :, 1, :, 1]
    )


def angles(frequencies, points, length):
    product = jnp.mod(frequencies[:, None] * points[None, :], length)
    return product.astype(jnp.float32) * (2.0 * math.pi / length)


def centered(number):
    return jnp.arange(number, dtype=jnp.int32) - number // 2


def forward_east_table(points, length, mode_count):
    phases = angles(centered(mode_count), points, length)
    factor = 1.0 / math.sqrt(length)
    return (jnp.stack([jnp.cos(phases).T, -jnp.sin(phases).T], axis=1) * factor).astype(
        jnp.bfloat16
    )


def forward_north_table(points, length, mode_count):
    phases = angles(centered(mode_count), points, length)
    factor = 1.0 / math.sqrt(length)
    cosines = jnp.cos(phases).T * factor
    sines = jnp.sin(phases).T * factor
    return jnp.stack(
        [jnp.concatenate([cosines, -sines], axis=1), jnp.concatenate([sines, cosines], axis=1)],
        axis=0,
    )


def inverse_north_table(points, length, mode_count):
    phases = angles(centered(mode_count), points, length)
    factor = 1.0 / math.sqrt(length)
    cosines = jnp.cos(phases) * factor
    sines = jnp.sin(phases) * factor
    return jnp.concatenate(
        [jnp.stack([cosines, sines], axis=1), jnp.stack([-sines, cosines], axis=1)], axis=0
    )


def inverse_east_table(points, length, mode_count):
    phases = angles(centered(mode_count), points, length)
    factor = 1.0 / math.sqrt(length)
    return jnp.stack([jnp.cos(phases) * factor, -jnp.sin(phases) * factor], axis=1)


def forward_depth_blocks(values, points, frequencies, length):
    slot_count = frequencies.shape[0]
    phases = angles(frequencies.reshape(-1), points, length).reshape(
        slot_count, frequencies.shape[1], points.shape[0]
    )
    factor = 1.0 / math.sqrt(length)
    cosines = jnp.cos(phases) * factor
    sines = jnp.sin(phases) * factor
    halfway = values.shape[-1] // 2
    real_in = values[..., :halfway]
    imag_in = values[..., halfway:]
    real_part = jnp.einsum("zcrbn,rkz->rkcbn", real_in, cosines, precision=highest) + jnp.einsum(
        "zcrbn,rkz->rkcbn", imag_in, sines, precision=highest
    )
    imag_part = jnp.einsum("zcrbn,rkz->rkcbn", imag_in, cosines, precision=highest) - jnp.einsum(
        "zcrbn,rkz->rkcbn", real_in, sines, precision=highest
    )
    return jnp.concatenate([real_part, imag_part], axis=-1)


def mix_channels(coeffs, weight):
    halfway = coeffs.shape[-1] // 2
    real_in = coeffs[..., :halfway]
    imag_in = coeffs[..., halfway:]
    weight_real = weight[..., :halfway]
    weight_imag = weight[..., halfway:]
    real_part = jnp.einsum(
        "kcmn,kmcon->komn", real_in, weight_real, precision=highest
    ) - jnp.einsum("kcmn,kmcon->komn", imag_in, weight_imag, precision=highest)
    imag_part = jnp.einsum(
        "kcmn,kmcon->komn", imag_in, weight_real, precision=highest
    ) + jnp.einsum("kcmn,kmcon->komn", real_in, weight_imag, precision=highest)
    return jnp.concatenate([real_part, imag_part], axis=-1)


def inverse_depth(values, frequencies, points, length):
    phases = angles(frequencies, points, length)
    factor = 1.0 / math.sqrt(length)
    cosines = jnp.cos(phases) * factor
    sines = jnp.sin(phases) * factor
    halfway = values.shape[-1] // 2
    real_in = values[..., :halfway]
    imag_in = values[..., halfway:]
    real_part = jnp.einsum("komn,kz->zomn", real_in, cosines, precision=highest) - jnp.einsum(
        "komn,kz->zomn", imag_in, sines, precision=highest
    )
    imag_part = jnp.einsum("komn,kz->zomn", imag_in, cosines, precision=highest) + jnp.einsum(
        "komn,kz->zomn", real_in, sines, precision=highest
    )
    return jnp.concatenate([real_part, imag_part], axis=-1)


def shards(fields, stiffness, lift_weight, lift_bias, mix_weight, spectral_weight, output_bias):
    east_tiles = lax.axis_size("gx")
    north_tiles = lax.axis_size("gy")
    depth_groups = lax.axis_size("ga")
    stacked = jnp.concatenate([fields, stiffness[None]], axis=0)
    padded = padded_2(stacked, (("gx", 2), ("gy", 3), ("ga", 1)), STEPS)
    fields_now = padded[:5]
    for repeat in range(STEPS):
        fields_now = step_interior(fields_now, trim(padded[5], repeat + 1))
    filtered = coarsen(fields_now)
    pre_lift = (
        jnp.einsum("fzxy,fc->zcxy", filtered, lift_weight, precision=highest)
        + lift_bias[None, :, None, None]
    )
    lifted = jax.nn.gelu(pre_lift, approximate=True).astype(jnp.bfloat16)
    depth_local = lifted.shape[0]
    length_east = lifted.shape[2] * east_tiles
    length_north = lifted.shape[3] * north_tiles
    length_depth = depth_local * depth_groups
    east_points = jnp.arange(length_east, dtype=jnp.int32)
    north_points = jnp.arange(length_north, dtype=jnp.int32)
    table_east = forward_east_table(east_points, length_east, MX)
    table_north = forward_north_table(north_points, length_north, MY)
    planes = lax.all_to_all(
        lax.all_to_all(lifted, "gx", split_axis=1, concat_axis=2, tiled=True),
        "gy",
        split_axis=0,
        concat_axis=3,
        tiled=True,
    )
    east_modes = jnp.einsum(
        "zcxy,xpm->zcpmy", planes, table_east, preferred_element_type=jnp.float32
    )
    north_modes = jnp.einsum("zcpmy,pyq->zcmq", east_modes, table_north, precision=highest)
    plane_count = planes.shape[0]
    depth_points = (
        lax.axis_index("ga") * depth_local
        + lax.axis_index("gy") * plane_count
        + jnp.arange(plane_count, dtype=jnp.int32)
    )
    block_east = MX // north_tiles
    block_depth = MZ // depth_groups
    grouped = north_modes.reshape(
        plane_count, north_modes.shape[1], north_tiles, block_east, 2 * MY
    )
    owners = jnp.arange(1 * lax.axis_size(("gy", "ga")), dtype=jnp.int32)
    picked = jnp.take(grouped, owners // depth_groups, axis=2)
    frequencies = (owners % depth_groups)[:, None] * block_depth + jnp.arange(
        block_depth, dtype=jnp.int32
    )[None, :]
    coeffs = lax.psum_scatter(
        forward_depth_blocks(picked, depth_points, frequencies, length_depth).astype(jnp.bfloat16),
        ("gy", "ga"),
        scatter_dimension=0,
        tiled=True,
    ).astype(jnp.float32)[0]
    mixed_modes = mix_channels(lax.all_gather(coeffs, "gx", axis=1, tiled=True), spectral_weight)
    own_frequencies = lax.axis_index("ga") * coeffs.shape[0] + jnp.arange(
        coeffs.shape[0], dtype=jnp.int32
    )
    points = jnp.arange(depth_local * lax.axis_size("ga"), dtype=jnp.int32)
    back_depth = lax.psum_scatter(
        inverse_depth(mixed_modes, own_frequencies, points, length_depth),
        "ga",
        scatter_dimension=0,
        tiled=True,
    )
    back_north = jnp.einsum(
        "zomq,qpy->zompy",
        back_depth,
        inverse_north_table(north_points, length_north, MY),
        precision=highest,
    )
    all_modes = lax.all_to_all(back_north, "gy", split_axis=4, concat_axis=2, tiled=True)
    spectral = jnp.einsum(
        "zompy,mpx->zoxy",
        all_modes,
        inverse_east_table(east_points, length_east, MX),
        precision=highest,
    ).astype(jnp.bfloat16)
    spectral = lax.all_to_all(spectral, "gx", split_axis=2, concat_axis=1, tiled=True)
    direct = jnp.einsum("zcxy,co->zoxy", lifted, mix_weight, preferred_element_type=jnp.float32)
    summed = direct + output_bias[None, :, None, None] + spectral.astype(jnp.float32)
    return jax.nn.gelu(summed, approximate=True).astype(jnp.bfloat16)


def solution(mesh):
    placed = (
        P(None, "ga", "gx", "gy"),
        P("ga", "gx", "gy"),
        P(),
        P(),
        P(),
        P("ga", "gy", None, "gx", None),
        P(),
    )
    return jax.shard_map(
        shards, mesh=mesh, in_specs=placed, out_specs=P("ga", None, "gx", "gy"), check_vma=False
    )
```

profile of v0, /device:TPU:0, one launch (start us, length us, event | category | flops | bytes accessed | tf_op | source)
XLA Modules:
  0.0 479.2 jit_solution(17202555115786274294)
XLA Ops:
  6.5 1.2 fusion.67
  7.8 3.0 collective-permute-start
  12.9 4.0 copy.86
  16.8 4.0 copy.85
  20.8 4.0 copy.87
  24.8 1.4 pad_maximum_fusion.7
  26.2 2.1 collective-permute-start.2
  28.3 2.3 collective-permute-start.3
  30.5 2.7 collective-permute-done.2
  33.5 6.5 %pad_maximum_fusion = f32[6,8,22,262]{2,1,3,0:T(8,128)S(1)} fusion(f32[6,8,22,3]{2,1,3,0:T(8,128)S(1)} %collective-permute-done.3, f32[6,8,3,256]{2,1,3,0:T(8,128)S(1)} %copy-done.2, f32[6,8,16,256]{2,1,3,0:T(8,128)} %copy.86, f32[6,8,3,256]{2,1,3,0:T(8,128)} %copy.85, f32[6,8,22,3]{2,1,3,0:T(8,128)S(1)} %collective-permute-done.2), kind=kLoop, calls=%fused_computation.1 | loop fusion | flops 1106688 | bytes 2213376 | tf_op jit(solution)/shard_map/concatenate | solution.py:30
  40.0 3.1 fusion.167
  43.8 4.0 copy.88
  47.8 2.3 copy.89
  50.6 5.1 %copy.90 = f32[6,8,22,262]{3,2,1,0:T(8,128)S(1)} copy(f32[6,8,22,262]{2,1,3,0:T(8,128)} %copy-done.1) | data formatting | bytes 2213376 | tf_op jit(solution)/shard_map/concatenate | solution.py:30
  55.7 1.3 pad_maximum_fusion.1
  57.0 3.0 slice_subtract_fusion.2
  60.5 4.1 multiply_add_fusion
  64.6 2.5 slice_subtract_fusion.5
  67.5 3.3 multiply_add_fusion.1
  71.9 1.2 multiply_add_fusion.2
  73.1 5.5 %copy.91 = f32[5,8,16,256]{1,3,2,0:T(8,128)} copy(f32[5,8,16,256]{3,2,1,0:T(8,128)S(1)} %multiply_add_fusion.2) | data formatting | bytes 1310720 | tf_op jit(solution)/shard_map/add | solution.py:59
  78.6 10.9 %fusion = f32[5,8,8,1,128,1]{1,5,4,3,2,0:T(1,128)S(1)} fusion(f32[5,8,8,2,128,2]{1,5,4,3,2,0:T(2,128)} %bitcast.187), kind=kLoop, calls=%fused_computation.8 | loop fusion | flops 163840 | bytes 819200 | tf_op jit(solution)/shard_map/mul | solution.py:69
  89.5 1.1 copy.92
  90.7 1.3 fusion.29
  93.0 3.5 all-to-all-start
  96.5 8.4 %all-to-all-done = bf16[8,32,8,128]{3,2,0,1:T(8,128)(2,1)S(1)} async-done(((bf16[8,32,8,128]{3,2,0,1:T(8,128)(2,1)}), bf16[8,32,8,128]{3,2,0,1:T(8,128)(2,1)S(1)}, u32[]{:S(2)}, u32[]{:S(2)}) %all-to-all-start) | async-done | bytes 524320 | tf_op jit(solution)/shard_map/all_to_all | solution.py:197
  105.8 4.4 all-to-all-start.1
  110.7 1.1 fusion.83
  112.2 11.9 %all-to-all-done.1 = bf16[8,8,32,128]{3,2,1,0:T(8,128)(2,1)S(1)} async-done(((bf16[8,8,32,128]{3,2,1,0:T(8,128)(2,1)}), bf16[8,8,32,128]{3,2,1,0:T(8,128)(2,1)S(1)}, u32[]{:S(2)}, u32[]{:S(2)}) %all-to-all-start.1) | async-done | bytes 524320 | tf_op jit(solution)/shard_map/all_to_all | solution.py:196
  125.2 1.8 fusion.19
  128.3 2.4 fusion.56
  130.6 3.0 fusion.52
  133.6 3.3 fusion.14
  136.9 2.5 fusion.15
  141.2 29.5 %reduce-scatter.3.cloned.1.call-done = bf16[1,4,8,8,128]{4,3,2,1,0:T(8,128)(2,1)} async-done(((bf16[8,4,8,8,128]{4,3,2,1,0:T(8,128)(2,1)}), bf16[1,4,8,8,128]{4,3,2,1,0:T(8,128)(2,1)}) %reduce-scatter.3.cloned.1.call-update) | async-done | bytes 65552 | tf_op jit(solution)/shard_map/reduce_scatter | solution.py:223
  171.5 10.2 %all-gather = f32[1,4,32,8,128]{4,3,1,0,2:T(8,128)S(1)} all-gather(f32[1,4,8,8,128]{4,3,1,0,2:T(8,128)S(1)} %copy.100), channel_id=2, replica_groups=mesh['gx'=4,'gy'=4,'ga'=2] {'gx'}, dimensions={2}, use_global_device_ids=true | all-gather | bytes 655360 | tf_op jit(solution)/shard_map/all_gather | solution.py:229
  182.5 1.3 copy-done.3
  183.9 2.4 multiply_reduce_fusion.3
  191.5 5.3 %reduce-scatter.5.cloned.1.call-done = f32[8,8,8,128]{3,0,2,1:T(8,128)} async-done(((f32[16,8,8,128]{3,0,2,1:T(8,128)}), f32[8,8,8,128]{3,0,2,1:T(8,128)}) %reduce-scatter.5.cloned.1.call-update) | async-done | bytes 262160 | tf_op jit(solution)/shard_map/reduce_scatter | solution.py:234
  196.8 2.7 fusion.40
  199.5 23.9 %copy.102 = f32[8,8,8,2,512]{2,3,1,0,4:T(2,128)} copy(f32[8,8,8,2,512]{4,0,3,2,1:T(8,128)S(1)} %fusion.40) | data formatting | bytes 4194304 | tf_op jit(solution)/shard_map/zomq,qpy->zompy/dot_general | solution.py:240
  223.4 66.8 %reshape.480 = f32[4,1,131072]{2,1,0:T(1,128)S(1)} reshape(f32[512,8,8,2,8]{4,3,2,1,0:T(2,128)} %bitcast.185) | data formatting | bytes 4194304
  290.3 53.4 %all_to_all.63 = f32[4,1,131072]{2,1,0:T(1,128)} all-to-all(f32[4,1,131072]{2,1,0:T(1,128)S(1)} %reshape.480), channel_id=1, replica_groups=mesh['gx'=4,'gy'=4,'ga'=2] {'gy'}, dimensions={0} | all-to-all | bytes 4194304 | tf_op jit(solution)/shard_map/all_to_all | solution.py:246
  344.2 7.7 %reduce.8 = f32[4,131072]{1,0:T(4,128)S(1)} reduce(f32[4,1,131072]{2,1,0:T(1,128)} %all_to_all.63, f32[]{:T(128)} %broadcast.796), dimensions={1}, to_apply=%all_to_all.54.reduce_sub_computation | reduce | bytes 4194308 | tf_op jit(solution)/shard_map/all_to_all | solution.py:246
  351.9 65.7 %reshape.481 = f32[512,8,8,2,8]{4,3,2,1,0:T(2,128)} reshape(f32[4,131072]{1,0:T(4,128)S(1)} %reduce.8) | data formatting | bytes 4194304
  417.6 40.1 %copy.103 = f32[8,8,8,2,4,128]{5,2,4,3,1,0:T(8,128)S(1)} copy(f32[8,8,8,2,4,128]{2,3,1,0,5,4:T(2,128)} %bitcast.186) | data formatting | bytes 4194304 | tf_op jit(solution)/shard_map/all_to_all | solution.py:246
  457.7 1.1 fusion.16
  459.1 11.4 %all_to_all.64 = bf16[8,8,32,128]{3,1,0,2:T(8,128)(2,1)S(1)} all-to-all(bf16[8,8,32,128]{3,1,0,2:T(8,128)(2,1)S(1)} %copy.104), channel_id=1, replica_groups=mesh['gx'=4,'gy'=4,'ga'=2] {'gx'}, dimensions={2} | all-to-all | bytes 1048576 | tf_op jit(solution)/shard_map/all_to_all | solution.py:253
  (81 shorter events, 21.3 us)
Async XLA Ops:
  6.5 463.9 %copy-start = (bf16[32,32]{1,0:T(8,128)(2,1)S(1)}, bf16[32,32]{1,0:T(8,128)(2,1)}, u32[]{:S(2)}) copy-start(bf16[32,32]{1,0:T(8,128)(2,1)} %param.11) | copy-start | bytes 6148
  6.5 5.3 %copy-start.4 = (f32[5,8,16,256]{3,2,1,0:T(8,128)S(1)}, f32[5,8,16,256]{3,2,1,0:T(8,128)}, u32[]{:S(2)}) copy-start(f32[5,8,16,256]{3,2,1,0:T(8,128)} %param.7) | copy-start | bytes 1966084
  7.8 9.0 %collective-permute-start = (f32[6,8,3,256]{3,1,2,0:T(8,128)S(1)}, f32[6,8,3,256]{3,1,2,0:T(8,128)S(1)}, u32[]{:S(2)}, u32[]{:S(2)}) collective-permute-start(f32[6,8,3,256]{3,1,2,0:T(8,128)S(1)} %copy.159), channel_id=1, source_target_pairs={{0,8},{8,16},{16,24},{24,0},{1,9},{9,17},{17,25},{25,1},{2,10},{10... | collective-permute-start | bytes 442376 | tf_op jit(solution)/shard_map/ppermute | solution.py:26
  10.9 10.0 %collective-permute-start.1 = (f32[6,8,3,256]{3,1,2,0:T(8,128)S(1)}, f32[6,8,3,256]{3,1,2,0:T(8,128)S(1)}, u32[]{:S(2)}, u32[]{:S(2)}) collective-permute-start(f32[6,8,3,256]{3,1,2,0:T(8,128)S(1)} %copy.160), channel_id=1, source_target_pairs={{8,0},{16,8},{24,16},{0,24},{9,1},{17,9},{25,17},{1,25},{10,2},{18... | collective-permute-start | bytes 442376 | tf_op jit(solution)/shard_map/ppermute | solution.py:29
  24.8 8.7 %copy-start.2 = (f32[6,8,3,256]{2,1,3,0:T(8,128)S(1)}, f32[6,8,3,256]{2,1,3,0:T(8,128)}, u32[]{:S(2)}) copy-start(f32[6,8,3,256]{2,1,3,0:T(8,128)} %copy.87) | copy-start | bytes 442372
  26.2 7.0 %collective-permute-start.2 = (f32[6,8,22,3]{2,1,3,0:T(8,128)S(1)}, f32[6,8,22,3]{2,1,3,0:T(8,128)S(1)}, u32[]{:S(2)}, u32[]{:S(2)}) collective-permute-start(f32[6,8,22,3]{2,1,3,0:T(8,128)S(1)} %get-tuple-element.11), channel_id=1, source_target_pairs={{0,2},{2,4},{4,6},{6,0},{1,3},{3,5},{5,7},{7,1},{8,10},{10,12},{12... | collective-permute-start | bytes 38024 | tf_op jit(solution)/shard_map/ppermute | solution.py:26
  28.3 5.2 %collective-permute-start.3 = (f32[6,8,22,3]{2,1,3,0:T(8,128)S(1)}, f32[6,8,22,3]{2,1,3,0:T(8,128)S(1)}, u32[]{:S(2)}, u32[]{:S(2)}) collective-permute-start(f32[6,8,22,3]{2,1,3,0:T(8,128)S(1)} %get-tuple-element.12), channel_id=1, source_target_pairs={{2,0},{4,2},{6,4},{0,6},{3,1},{5,3},{7,5},{1,7},{10,8},{12,10},{14... | collective-permute-start | bytes 38024 | tf_op jit(solution)/shard_map/ppermute | solution.py:29
  40.0 3.7 copy-start.1
  47.8 7.9 %collective-permute-start.4 = (f32[6,3,22,262]{3,2,1,0:T(8,128)}, f32[6,3,22,262]{3,2,1,0:T(8,128)}, u32[]{:S(2)}, u32[]{:S(2)}) collective-permute-start(f32[6,3,22,262]{3,2,1,0:T(8,128)} %copy.88), channel_id=1, source_target_pairs={{0,1},{1,0},{2,3},{3,2},{4,5},{5,4},{6,7},{7,6},{8,9},{9,8},{10,11... | collective-permute-start | bytes 1245032 | tf_op jit(solution)/shard_map/ppermute | solution.py:26
  50.1 5.7 %collective-permute-start.5 = (f32[6,3,22,262]{3,2,1,0:T(8,128)}, f32[6,3,22,262]{3,2,1,0:T(8,128)S(1)}, u32[]{:S(2)}, u32[]{:S(2)}) collective-permute-start(f32[6,3,22,262]{3,2,1,0:T(8,128)} %copy.89), channel_id=1, source_target_pairs={{1,0},{0,1},{3,2},{2,3},{5,4},{4,5},{7,6},{6,7},{9,8},{8,9},{11,10... | collective-permute-start | bytes 1245032 | tf_op jit(solution)/shard_map/ppermute | solution.py:29
  89.5 1.2 copy-start.5
  89.5 1.2 copy-start.6
  93.0 11.9 %all-to-all-start = ((bf16[8,32,8,128]{3,2,0,1:T(8,128)(2,1)}), bf16[8,32,8,128]{3,2,0,1:T(8,128)(2,1)S(1)}, u32[]{:S(2)}, u32[]{:S(2)}) async-start(bf16[8,32,8,128]{3,2,0,1:T(8,128)(2,1)} %copy.94), calls=%async_computation | async-start | bytes 1048576 | tf_op jit(solution)/shard_map/all_to_all | solution.py:197
  105.8 18.2 %all-to-all-start.1 = ((bf16[8,8,32,128]{3,2,1,0:T(8,128)(2,1)}), bf16[8,8,32,128]{3,2,1,0:T(8,128)(2,1)S(1)}, u32[]{:S(2)}, u32[]{:S(2)}) async-start(bf16[8,8,32,128]{3,2,1,0:T(8,128)(2,1)} %bitcast.183), calls=%async_computation.1 | async-start | bytes 1048576 | tf_op jit(solution)/shard_map/all_to_all | solution.py:196
  110.3 60.4 %reduce-scatter.3.cloned.1.call-start = ((), (), s32[]{:S(2)}) async-start(), calls=%async_computation.6 | async-start | bytes 589824 | tf_op jit(solution)/shard_map/reduce_scatter | solution.py:223
  141.1 55.7 %reduce-scatter.5.cloned.1.call-start = ((), (), s32[]{:S(2)}) async-start(), calls=%async_computation.7 | async-start | bytes 786432 | tf_op jit(solution)/shard_map/reduce_scatter | solution.py:234
  181.7 2.2 copy-start.3
  457.7 12.7 %copy-start.7 = (f32[32]{0:T(128)S(1)}, f32[32]{0:T(128)}, u32[]{:S(2)}) copy-start(f32[32]{0:T(128)} %param.13) | copy-start | bytes 388
Sparse Core Ops, SparseCore 0:
  141.2 29.4 reduce-scatter.2
  191.0 5.7 reduce-scatter.4
where the time goes:
time: 483 us; the launch traced here: 479 us
  local copies, waits for them, and re-layouts  239 us (49%)
  blocking collectives  74.9 us (16%)
  waiting for transfers between devices  58.1 us (12%)
  other arithmetic  52.5 us (11%)
  matrix products  22.9 us (5%)
  starting transfers between devices  17.3 us (4%)
  between operations  14.2 us (3%)
    unnamed x32, local copies, waits for them, and re-layouts  136 us
    all_to_all x1, blocking collectives, shards(): lax.all_to_all(back_north, 'gy', split_axis=4, concat_axis=2, tiled=True)  53.4 us
    all_to_all x2, local copies, waits for them, and re-layouts, shards(): lax.all_to_all(back_north, 'gy', split_axis=4, concat_axis=2, tiled=True)  40.6 us
    reduce_scatter x1, waiting for transfers between devices, shards(): lax.psum_scatter(forward_depth_blocks(picked, depth_points, frequencies,...  29.5 us
    dot_general x1, local copies, waits for them, and re-layouts, shards(): jnp.einsum('zomq,qpy->zompy', back_depth, inverse_north_table(north_point...  23.9 us
    all_to_all x1, waiting for transfers between devices, shards(): lax.all_to_all(lax.all_to_all(lifted, 'gx', split_axis=1, concat_axis=2,...  11.9 us
    all_to_all x1, blocking collectives, shards(): lax.all_to_all(spectral, 'gx', split_axis=2, concat_axis=1, tiled=True)  11.4 us
    mul x1, other arithmetic, coarsen(): 0.25 * (blocks[:, :, :, 0, :, 0] + blocks[:, :, :, 1, :, 0] + blocks[:, :...  10.9 us
  transfers between devices with their start and end apart: 10, of which 6 were waited for; matrix products, arithmetic and copies ran while one was open for 4% of the time, Pallas kernels for 0%

commit v1 on v0

v1 whole, which is shorter than its diff:
```python
import math

import functools
import jax
import jax.numpy as jnp
import numpy as np
from jax import lax
from jax.experimental import pallas as pl
from jax.experimental.pallas import tpu as pltpu
from jax.sharding import PartitionSpec as P

STEPS = 3
MX = 32
MY = 64
MZ = 8


courant_half = 0.1
smooth_half = 0.15
mean_flow = (0.3, -0.2, 0.1)
highest = lax.Precision.HIGHEST


def padded_2(block, sides, width):
    for axis, dim in sides:
        count = lax.axis_size(axis)
        forward = [(i, i + 1) for i in range(count - 1)]
        forward.append((count - 1, 0))
        backward = [(target, source) for source, target in forward]
        low = lax.ppermute(
            lax.slice_in_dim(block, block.shape[dim] - width, None, axis=dim), axis, forward
        )
        high = lax.ppermute(lax.slice_in_dim(block, 0, width, axis=dim), axis, backward)
        block = jnp.concatenate([low, block, high], axis=dim)
    return block


def step_interior(padded, stiff_part):
    center = padded[:, 1:-1, 1:-1, 1:-1]
    upper_depth = padded[:, 2:, 1:-1, 1:-1]
    lower_depth = padded[:, :-2, 1:-1, 1:-1]
    upper_east = padded[:, 1:-1, 2:, 1:-1]
    lower_east = padded[:, 1:-1, :-2, 1:-1]
    upper_north = padded[:, 1:-1, 1:-1, 2:]
    lower_north = padded[:, 1:-1, 1:-1, :-2]
    slope_depth = upper_depth - lower_depth
    slope_east = upper_east - lower_east
    slope_north = upper_north - lower_north
    curvature = (
        upper_depth
        + lower_depth
        + upper_east
        + lower_east
        + upper_north
        + lower_north
        - 6.0 * center
    )
    transport = mean_flow[0] * slope_east + mean_flow[1] * slope_north + mean_flow[2] * slope_depth
    diverge = slope_east[1] + slope_north[2] + slope_depth[3]
    coupling = jnp.stack(
        [diverge, slope_east[4], slope_north[4], slope_depth[4], stiff_part * diverge]
    )
    return center - courant_half * (transport + coupling) + smooth_half * curvature


def trim(block, margin):
    return block[margin:-margin, margin:-margin, margin:-margin]


def coarsen(fields_now):
    extent = fields_now.shape
    blocks = fields_now.reshape(extent[0], extent[1], extent[2] // 2, 2, extent[3] // 2, 2)
    return 0.25 * (
        blocks[:, :, :, 0, :, 0]
        + blocks[:, :, :, 1, :, 0]
        + blocks[:, :, :, 0, :, 1]
        + blocks[:, :, :, 1, :, 1]
    )


def angles(frequencies, points, length):
    product = jnp.mod(frequencies[:, None] * points[None, :], length)
    return product.astype(jnp.float32) * (2.0 * math.pi / length)


def centered(number):
    return jnp.arange(number, dtype=jnp.int32) - number // 2


MESH = pl.DeviceIdType.MESH
f32 = jnp.float32
bf16 = jnp.bfloat16


def gelu(v):
    return 0.5 * v * (1.0 + jnp.tanh(math.sqrt(2.0 / math.pi) * (v + 0.044715 * (v * v * v))))


def swapped(v):
    sign = jnp.where(lax.broadcasted_iota(jnp.int32, (v.shape[0], 2 * MY), 1) < MY, 1.0, -1.0)
    parts = [
        pltpu.roll(v[:, i : i + 2 * MY], MY, 1) * sign for i in range(0, v.shape[1], 2 * MY)
    ]
    return jnp.concatenate(parts, axis=1) if len(parts) > 1 else parts[0]


def dot(a, b, dims=((1,), (0,))):
    return lax.dot_general(a, b, (dims, ((), ())), preferred_element_type=f32)


def peers(axis):
    count = lax.axis_size(axis)
    me = lax.axis_index(axis)
    return me, [(d, lax.rem(me + d, count), lax.rem(me + count - d, count)) for d in range(1, count)]


def remote(src, dst, sems, slot, axis, peer):
    return pltpu.make_async_remote_copy(
        src_ref=src,
        dst_ref=dst,
        send_sem=sems[0].at[slot],
        recv_sem=sems[1].at[slot],
        device_id={axis: peer},
        device_id_type=MESH,
    )


def layer_kernel(
    cfg,
    filt, lw, lb, mixk, bias, base_e, base_d, cz, sz, x1, x2, w_hbm,
    out,
    lift, table, p_send, p_recv, p2, r2, q3, r3, c4, r4, rr, ii, mf, r5, r6, s7, r7, wv,
    wsem, s1s, s1r, s2s, s2r, s3s, s3r, s4s, s4r, s5s, s5r, s6s, s6r, s7s, s7r,
):
    G, H, C, CB, KB, OB, KZ, NZL, XL, YL = cfg
    Q = 2 * MY
    gx, gx_peers = peers("gx")
    gy, gy_peers = peers("gy")
    ga = lax.axis_index("ga")
    other = 1 - ga
    weights = pltpu.make_async_copy(w_hbm, wv, wsem)
    weights.start()
    barrier = pltpu.get_barrier_semaphore()
    for axis, group in (("gx", gx_peers), ("gy", gy_peers)):
        for _, peer, _ in group:
            pl.semaphore_signal(barrier, inc=1, device_id={axis: peer}, device_id_type=MESH)
    pl.semaphore_signal(barrier, inc=1, device_id={"ga": other}, device_id_type=MESH)

    e, d = base_e[...], base_d[...]
    for z in range(NZL):
        for k in range(2 * KZ):
            block = e * cz[z, k] + d * sz[z, k]
            table[k // KZ, z * YL : (z + 1) * YL, (k % KZ) * Q : (k % KZ + 1) * Q] = block.astype(bf16)

    def lift_two(pair, carry):
        c = pair * 2
        rows = pl.ds(pl.multiple_of(pair * 2 * XL, 2 * XL), 2 * XL)
        for z in range(NZL):
            halves = []
            for h in range(2):
                v = filt[0, z] * lw[0, c + h]
                for f in range(1, 5):
                    v = v + filt[f, z] * lw[f, c + h]
                halves.append(gelu(v + lb[c + h]))
            lift[rows, z * YL : (z + 1) * YL] = jnp.concatenate(halves, axis=0).astype(bf16)
        return carry

    lax.fori_loop(0, C // 2, lift_two, 0)
    pl.semaphore_wait(barrier, (G - 1) + (H - 1) + 1)

    p_send[...] = dot(lift[...], table[other]).astype(bf16)
    copy = remote(p_send, p_recv, (s1s, s1r), 0, "ga", other)
    copy.start()
    mine = dot(lift[...], table[ga])
    copy.wait()
    total = (mine + p_recv[...].astype(f32)).astype(bf16)
    p2[...] = total.reshape(p2.shape)

    copies = []
    for n, peer, _ in gx_peers:
        copies.append(remote(p2.at[peer], r2.at[gx], (s2s, s2r), n - 1, "gx", peer))
        copies[-1].start()
    r2[gx] = p2[gx]
    for one in copies:
        one.wait()
    v = r2[...].reshape(C * XL, KZ * Q)
    vs = swapped(v.astype(f32)).astype(bf16)
    q3[...] = dot(x1[...], jnp.concatenate([v, vs], axis=0)).astype(bf16).reshape(q3.shape)

    copies = []
    for n, peer, _ in gy_peers:
        copies.append(remote(q3.at[peer], r3.at[n - 1], (s3s, s3r), n - 1, "gy", peer))
        copies[-1].start()
    acc = q3[gy].astype(f32)
    for n, one in enumerate(copies):
        one.wait()
        acc = acc + r3[n].astype(f32)
    c4[...] = acc.astype(bf16)

    copies = []
    for n, peer, _ in gx_peers:
        copies.append(remote(c4, r4.at[gx], (s4s, s4r), n - 1, "gx", peer))
        copies[-1].start()
    r4[gx] = c4[...]
    for one in copies:
        one.wait()
    v = r4[...].reshape(C * KB, KZ * Q).astype(f32)
    low = lax.broadcasted_iota(jnp.int32, (C * KB, Q), 1) < MY
    for k in range(KZ):
        part = v[:, k * Q : (k + 1) * Q]
        turned = pltpu.roll(part, MY, 1)
        rr[k] = jnp.where(low, part, turned)
        ii[k] = jnp.where(low, turned, part)
    weights.wait()

    def mix_one(kx, carry):
        for k in range(KZ):
            lanes = slice(k * Q, (k + 1) * Q)
            a = jnp.zeros((OB, Q), f32)
            b = jnp.zeros((OB, Q), f32)
            for c in range(C):
                w = wv[k, kx, c]
                a = a + w * rr[k, pl.ds(c * KB + kx, 1), :]
                b = b + w * ii[k, pl.ds(c * KB + kx, 1), :]
            mf[kx, :, lanes] = a - swapped(b)
        return carry

    lax.fori_loop(0, KB, mix_one, 0)

    r5[gy] = mf[...].reshape(KB * OB, KZ * Q).astype(bf16)
    copies = []
    for n, peer, _ in gy_peers:
        copies.append(remote(r5.at[gy], r5.at[gy], (s5s, s5r), n - 1, "gy", peer))
        copies[-1].start()
    forwards = [remote(r5.at[gy], r6.at[gy], (s6s, s6r), 0, "ga", other)]
    forwards[0].start()
    for (n, _, source), one in zip(gy_peers, copies):
        one.wait_recv()
        forwards.append(remote(r5.at[source], r6.at[source], (s6s, s6r), n, "ga", other))
        forwards[-1].start()

    def back(v):
        vs = swapped(v.astype(f32)).astype(bf16)
        return dot(x2[...], jnp.concatenate([v, vs], axis=0)).astype(bf16)

    rows = H * KB * OB
    y_mine = back(r5[...].reshape(rows, KZ * Q))
    spec = dot(y_mine, table[ga], ((1,), (1,)))
    for one in copies:
        one.wait_send()
    for one in forwards:
        one.wait()
    y_other = back(r6[...].reshape(rows, KZ * Q))
    spec = spec + dot(y_other, table[other], ((1,), (1,)))
    s7[...] = spec.astype(bf16).reshape(s7.shape)

    copies = []
    for n, peer, _ in gx_peers:
        copies.append(remote(s7.at[peer], r7.at[gx], (s7s, s7r), n - 1, "gx", peer))
        copies[-1].start()
    r7[gx] = s7[gx]
    direct = dot(mixk[...], lift[...]) + bias[...]
    for one in copies:
        one.wait()
    for z in range(NZL):
        lanes = slice(z * YL, (z + 1) * YL)
        both = direct[:, lanes] + r7[:, :, lanes].reshape(C * XL, YL).astype(f32)
        out[z] = gelu(both).astype(bf16).reshape(C, XL, YL)


def east_tables(G, H, XL, C):
    CB, KB, OB = C // G, MX // H, C // G
    length = G * XL
    k = np.arange(MX) - MX // 2
    ang = 2.0 * np.pi * ((k[:, None] * np.arange(length)[None, :]) % length) / length
    scale = 1.0 / math.sqrt(length)
    cos, sin = np.cos(ang) * scale, np.sin(ang) * scale
    cos[np.abs(cos) < 1e-12] = 0.0
    sin[np.abs(sin) < 1e-12] = 0.0

    def forward(t):
        t = t.reshape(H, KB, G, XL)
        full = np.einsum("hkgx,cd->hckgdx", t, np.eye(CB))
        return full.reshape(H * CB * KB, G * CB * XL)

    def inverse(t):
        t = t.reshape(H, KB, G, XL)
        full = np.einsum("hkgx,op->goxhkp", t, np.eye(OB))
        return full.reshape(G * OB * XL, H * KB * OB)

    x1 = np.concatenate([forward(cos), forward(sin)], axis=1)
    x2 = np.concatenate([inverse(cos), -inverse(sin)], axis=1)
    return jnp.asarray(x1, bf16), jnp.asarray(x2, bf16)


def shards(fields, stiffness, lift_weight, lift_bias, mix_weight, spectral_weight, output_bias):
    G, H, A = (lax.axis_size(n) for n in ("gx", "gy", "ga"))
    stacked = jnp.concatenate([fields, stiffness[None]], axis=0)
    padded = padded_2(stacked, (("gx", 2), ("gy", 3), ("ga", 1)), STEPS)
    fields_now = padded[:5]
    for repeat in range(STEPS):
        fields_now = step_interior(fields_now, trim(padded[5], repeat + 1))
    filtered = coarsen(fields_now)
    _, NZL, XL, YL = filtered.shape
    C = lift_weight.shape[1]
    CB, KB, OB, KZ, Q = C // G, MX // H, C // G, MZ // A, 2 * MY
    length_z, length_y = NZL * A, YL * H
    y_points = lax.axis_index("gy") * YL + jnp.arange(YL, dtype=jnp.int32)
    u = angles(centered(MY), y_points, length_y).T
    scale = 1.0 / math.sqrt(length_y * length_z)
    cu, su = jnp.cos(u) * scale, jnp.sin(u) * scale
    base_e = jnp.concatenate([cu, -su], axis=1)
    base_d = jnp.concatenate([-su, -cu], axis=1)
    z_points = lax.axis_index("ga") * NZL + jnp.arange(NZL, dtype=jnp.int32)
    v = angles(jnp.arange(MZ, dtype=jnp.int32), z_points, length_z).T
    x1, x2 = east_tables(G, H, XL, C)
    mixk = jnp.kron(mix_weight.T, jnp.eye(XL, dtype=bf16))
    bias = jnp.repeat(output_bias, XL)[:, None]
    cfg = (G, H, C, CB, KB, OB, KZ, NZL, XL, YL)
    vmem = pl.BlockSpec(memory_space=pltpu.VMEM)
    smem = pl.BlockSpec(memory_space=pltpu.SMEM)
    hbm = pl.BlockSpec(memory_space=pl.ANY)
    L = KZ * Q
    dma = pltpu.SemaphoreType.DMA
    V = pltpu.VMEM
    return pl.pallas_call(
        functools.partial(layer_kernel, cfg),
        out_shape=jax.ShapeDtypeStruct((NZL, C, XL, YL), bf16),
        in_specs=[vmem, smem, smem, vmem, vmem, vmem, vmem, smem, smem, vmem, vmem, hbm],
        out_specs=vmem,
        scratch_shapes=[
            V((C * XL, NZL * YL), bf16),
            V((A, NZL * YL, L), bf16),
            V((C * XL, L), bf16),
            V((C * XL, L), bf16),
            V((G, CB * XL, L), bf16),
            V((G, CB * XL, L), bf16),
            V((H, CB * KB, L), bf16),
            V((H - 1, CB * KB, L), bf16),
            V((CB * KB, L), bf16),
            V((G, CB * KB, L), bf16),
            V((KZ, C * KB, Q), f32),
            V((KZ, C * KB, Q), f32),
            V((KB, OB, L), f32),
            V((H, KB * OB, L), bf16),
            V((H, KB * OB, L), bf16),
            V((G, OB * XL, NZL * YL), bf16),
            V((G, OB * XL, NZL * YL), bf16),
            V(spectral_weight.shape, f32),
            dma,
            dma((1,)), dma((1,)),
            dma((G - 1,)), dma((G - 1,)),
            dma((H - 1,)), dma((H - 1,)),
            dma((G - 1,)), dma((G - 1,)),
            dma((H - 1,)), dma((H - 1,)),
            dma((H,)), dma((H,)),
            dma((G - 1,)), dma((G - 1,)),
        ],
        compiler_params=pltpu.CompilerParams(collective_id=0, has_side_effects=True, vmem_limit_bytes=48 * 2**20),
    )(
        filtered, lift_weight, lift_bias, mixk, bias, base_e, base_d,
        jnp.cos(v), jnp.sin(v), x1, x2, spectral_weight,
    )


def solution(mesh):
    placed = (
        P(None, "ga", "gx", "gy"),
        P("ga", "gx", "gy"),
        P(),
        P(),
        P(),
        P("ga", "gy", None, "gx", None),
        P(),
    )
    return jax.shard_map(
        shards, mesh=mesh, in_specs=placed, out_specs=P("ga", None, "gx", "gy"), check_vma=False
    )
```

time: 483 us -> 151 us (0.31)
  local copies, waits for them, and re-layouts: 239 us -> 69.8 us
  blocking collectives: 74.9 us -> 0 us
  waiting for transfers between devices: 58.1 us -> 0.02 us
  Pallas kernels: 0 us -> 38.7 us
  matrix products: 22.9 us -> 0 us
  other arithmetic: 52.5 us -> 32 us
  between operations: 14.2 us -> 0.39 us
  starting transfers between devices: 17.3 us -> 8.86 us
    unnamed x32 -> x34, local copies, waits for them, and re-layouts: 136 us -> 19.9 us
    all_to_all x2 -> x0, blocking collectives: 64.8 us -> none  [the longest x1 53.4 us: shards(): lax.all_to_all(back_north, 'gy', split_axis=4, concat_axis=2, tiled=True)]
    all_to_all x5 -> x0, local copies, waits for them, and re-layouts: 42.1 us -> none  [the longest x2 40.6 us: shards(): lax.all_to_all(back_north, 'gy', split_axis=4, concat_axis=2, tiled=True)]
    pallas_call x0 -> x1, Pallas kernels: none -> 38.7 us  [shards(): pl.pallas_call(functools.partial(layer_kernel, cfg), out_shape=jax.ShapeD...]
    reduce_scatter x2 -> x0, waiting for transfers between devices: 34.8 us -> none  [the longest x1 29.5 us: shards(): lax.psum_scatter(forward_depth_blocks(picked, depth_points, frequencies,...]
    dot_general x1 -> x0, local copies, waits for them, and re-layouts: 23.9 us -> none  [shards(): jnp.einsum('zomq,qpy->zompy', back_depth, inverse_north_table(north_point...]
    dot_general x14 -> x0, matrix products: 22.9 us -> none  [the longest x1 3.32 us: forward_depth_blocks(): jnp.einsum('zcrbn,rkz->rkcbn', imag_in, sines, precision=highest)]
    all_to_all x2 -> x0, waiting for transfers between devices: 20.3 us -> none  [the longest x1 11.9 us: shards(): lax.all_to_all(lax.all_to_all(lifted, 'gx', split_axis=1, concat_axis=2,...]
  transfers between devices with their start and end apart: 10 -> 6, of which waited for: 6 -> 0; matrix products, arithmetic and copies ran while one was open for 4% -> 15% of each run, Pallas kernels for 0% -> 0%
where the time goes in v1:
time: 151 us; the launch traced here: 150 us
  local copies, waits for them, and re-layouts  69.8 us (46%)
  Pallas kernels  38.7 us (26%)
  other arithmetic  32 us (21%)
  starting transfers between devices  8.86 us (6%)
    pallas_call x1, Pallas kernels, shards(): pl.pallas_call(functools.partial(layer_kernel, cfg), out_shape=jax.ShapeD...  38.7 us
    unnamed x34, local copies, waits for them, and re-layouts  19.9 us
    slice x1, local copies, waits for them, and re-layouts, coarsen(): blocks[:, :, :, 1, :, 0]  14.6 us
    concatenate x2, other arithmetic, padded_2(): block = jnp.concatenate([low, block, high], axis=dim)  9.48 us
    add x3, other arithmetic, step_interior(): center - courant_half * (transport + coupling) + smooth_half * curvature  8.56 us
    slice x2, local copies, waits for them, and re-layouts, padded_2(): lax.slice_in_dim(block, block.shape[dim] - width, None, axis=dim)  7.2 us
    sub x3, other arithmetic, step_interior(): slope_east = upper_east - lower_east  6.44 us
    add x1, local copies, waits for them, and re-layouts, step_interior(): center - courant_half * (transport + coupling) + smooth_half * curvature  5.52 us
  transfers between devices with their start and end apart: 6, of which 0 were waited for; matrix products, arithmetic and copies ran while one was open for 15% of the time, Pallas kernels for 0%

profile of v1, /device:TPU:0, one launch (start us, length us, event | category | flops | bytes accessed | tf_op | source)
XLA Modules:
  0.0 149.8 jit_solution(17183564311262119889)
XLA Ops:
  0.0 1.2 fusion.4
  1.3 3.0 %collective-permute-start = (f32[6,8,3,256]{3,1,2,0:T(8,128)S(1)}, f32[6,8,3,256]{3,1,2,0:T(8,128)S(1)}, u32[]{:S(2)}, u32[]{:S(2)}) collective-permute-start(f32[6,8,3,256]{3,1,2,0:T(8,128)S(1)} %copy.59), channel_id=1, source_target_pairs={{0,8},{8,16},{16,24},{24,0},{1,9},{9,17},{17,25},{25,1},{2,10},{10... | collective-permute-start | bytes 442376 | tf_op jit(solution)/shard_map/ppermute | solution.py:30
  4.3 0.7 copy.60
  5.0 1.0 collective-permute-start.1
  5.9 1.0 pad_maximum_fusion.2
  6.9 0.1 copy.57
  7.0 0.2 broadcast_multiply_fusion
  7.2 4.0 %copy.47 = f32[6,8,16,256]{2,1,3,0:T(8,128)} copy(f32[6,8,16,256]{3,2,1,0:T(8,128)S(1)} %pad_maximum_fusion.2) | data formatting | bytes 1572864 | tf_op jit(solution)/shard_map/concatenate | solution.py:298
  11.3 4.0 %copy.46 = f32[6,8,3,256]{2,1,3,0:T(8,128)} copy(f32[6,8,3,256]{3,1,2,0:T(8,128)S(1)} %collective-permute-done) | data formatting | bytes 294912 | tf_op jit(solution)/shard_map/ppermute | solution.py:30
  15.3 4.0 %copy.48 = f32[6,8,3,256]{2,1,3,0:T(8,128)} copy(f32[6,8,3,256]{3,1,2,0:T(8,128)S(1)} %collective-permute-done.1) | data formatting | bytes 294912 | tf_op jit(solution)/shard_map/ppermute | solution.py:33
  19.3 1.2 pad_maximum_fusion.5
  20.5 2.1 %collective-permute-start.2 = (f32[6,8,22,3]{2,1,3,0:T(8,128)S(1)}, f32[6,8,22,3]{2,1,3,0:T(8,128)S(1)}, u32[]{:S(2)}, u32[]{:S(2)}) collective-permute-start(f32[6,8,22,3]{2,1,3,0:T(8,128)S(1)} %get-tuple-element.5), channel_id=1, source_target_pairs={{0,2},{2,4},{4,6},{6,0},{1,3},{3,5},{5,7},{7,1},{8,10},{10,12},{12... | collective-permute-start | bytes 38024 | tf_op jit(solution)/shard_map/ppermute | solution.py:30
  22.6 2.3 %collective-permute-start.3 = (f32[6,8,22,3]{2,1,3,0:T(8,128)S(1)}, f32[6,8,22,3]{2,1,3,0:T(8,128)S(1)}, u32[]{:S(2)}, u32[]{:S(2)}) collective-permute-start(f32[6,8,22,3]{2,1,3,0:T(8,128)S(1)} %get-tuple-element.6), channel_id=1, source_target_pairs={{2,0},{4,2},{6,4},{0,6},{3,1},{5,3},{7,5},{1,7},{10,8},{12,10},{14... | collective-permute-start | bytes 38024 | tf_op jit(solution)/shard_map/ppermute | solution.py:33
  24.8 1.0 fusion.11
  25.8 2.8 %mul.224.mixk = bf16[256,256]{1,0:T(8,128)(2,1)S(1)} reshape(bf16[32,8,32,8]{3,2,1,0:T(8,128)(2,1)S(1)} %broadcast_multiply_fusion) | data formatting | bytes 262144 | tf_op jit(solution)/shard_map/jit(kron)/mul | solution.py:317
  28.7 0.1 broadcast_in_dim.9
  28.8 0.1 broadcast_in_dim_reshape.4.bias
  28.9 8.2 %pad_maximum_fusion = f32[6,8,22,262]{2,1,3,0:T(8,128)S(1)} fusion(f32[6,8,22,3]{2,1,3,0:T(8,128)S(1)} %collective-permute-done.3, f32[6,8,3,256]{2,1,3,0:T(8,128)} %copy.48, f32[6,8,16,256]{2,1,3,0:T(8,128)} %copy.47, f32[6,8,3,256]{2,1,3,0:T(8,128)} %copy.46, f32[6,8,22,3]{2,1,3,0:T(8,128)S(1)} %collective-permute-done.2), kind=kLoop, calls=%fused_computation | loop fusion | flops 1106688 | bytes 2213376 | tf_op jit(solution)/shard_map/concatenate | solution.py:34
  37.1 3.2 %fusion.22 = (f32[6,3,22,262]{2,1,3,0:T(4,128)}, f32[6,3,22,262]{2,1,3,0:T(4,128)S(1)}) fusion(f32[6,8,22,262]{2,1,3,0:T(8,128)S(1)} %pad_maximum_fusion), kind=kLoop, calls=%fused_computation.84 | loop fusion | bytes 1660032 | tf_op jit(solution)/shard_map/slice | solution.py:31
  40.3 0.5 copy-done.5
  40.8 4.0 %copy.49 = f32[6,3,22,262]{3,2,1,0:T(8,128)} copy(f32[6,3,22,262]{2,1,3,0:T(4,128)} %get-tuple-element.11) | data formatting | bytes 830016 | tf_op jit(solution)/shard_map/slice | solution.py:31
  44.8 2.3 %copy.50 = f32[6,3,22,262]{3,2,1,0:T(8,128)} copy(f32[6,3,22,262]{2,1,3,0:T(4,128)S(1)} %get-tuple-element.12) | data formatting | bytes 830016 | tf_op jit(solution)/shard_map/slice | solution.py:33
  47.1 0.5 collective-permute-start.5
  47.6 1.0 pad_maximum_fusion.7
  48.7 0.1 fusion.19
  48.8 5.1 %copy.51 = f32[6,8,22,262]{3,2,1,0:T(8,128)S(1)} copy(f32[6,8,22,262]{2,1,3,0:T(8,128)} %copy-done.5) | data formatting | bytes 2213376 | tf_op jit(solution)/shard_map/concatenate | solution.py:34
  53.9 1.3 pad_maximum_fusion.1
  55.2 3.0 %slice_subtract_fusion.2 = (f32[5,12,20,260]{3,2,1,0:T(8,128)S(1)}, f32[5,12,20,260]{3,2,1,0:T(8,128)S(1)}, f32[5,12,20,260]{3,2,1,0:T(8,128)S(1)}) fusion(f32[6,14,22,262]{3,2,1,0:T(8,128)S(1)} %pad_maximum_fusion.1), kind=kLoop, calls=%fused_computation.5 | loop fusion | flops 936000 | bytes 11232000 | tf_op jit(solution)/shard_map/sub | solution.py:47
  58.3 0.1 constant_dynamic-update-slice_fusion
  58.5 0.2 fusion.1
  58.6 4.1 %multiply_add_fusion = f32[5,12,20,260]{3,2,1,0:T(8,128)S(1)} fusion(f32[6,14,22,262]{3,2,1,0:T(8,128)S(1)} %pad_maximum_fusion.1, f32[5,12,20,260]{3,2,1,0:T(8,128)S(1)} %fusion.1, f32[5,12,20,260]{3,2,1,0:T(8,128)S(1)} %get-tuple-element.15, f32[5,12,20,260]{3,2,1,0:T(8,128)S(1)} %get-tuple-element.14, f32[5,12,20,260]{3,2,1,0:T(8,128)S(1)} %get-tuple-element.13), kind=kLoop, calls=%fused_computation.2 | loop fusion | flops 5304000 | bytes 14976000 | tf_op jit(solution)/shard_map/add | solution.py:63
  62.8 2.5 %slice_subtract_fusion.5 = (f32[5,10,18,258]{3,2,1,0:T(8,128)S(1)}, f32[5,10,18,258]{3,2,1,0:T(8,128)S(1)}, f32[5,10,18,258]{3,2,1,0:T(8,128)S(1)}) fusion(f32[5,12,20,260]{3,2,1,0:T(8,128)S(1)} %multiply_add_fusion), kind=kLoop, calls=%fused_computation.9 | loop fusion | flops 696600 | bytes 8359200 | tf_op jit(solution)/shard_map/sub | solution.py:47
  65.3 0.1 constant_dynamic-update-slice_fusion.1
  65.5 0.2 fusion.3
  65.6 3.3 %multiply_add_fusion.1 = f32[5,10,18,258]{3,2,1,0:T(8,128)S(1)} fusion(f32[5,12,20,260]{3,2,1,0:T(8,128)S(1)} %multiply_add_fusion, f32[5,10,18,258]{3,2,1,0:T(8,128)S(1)} %fusion.3, f32[5,10,18,258]{3,2,1,0:T(8,128)S(1)} %get-tuple-element.17, f32[5,10,18,258]{3,2,1,0:T(8,128)S(1)} %get-tuple-element.18, f32[5,10,18,258]{3,2,1,0:T(8,128)S(1)} %get-tuple-element.16), kind=kLoop, calls=%fused_computation.6 | loop fusion | flops 3947400 | bytes 11145600 | tf_op jit(solution)/shard_map/add | solution.py:63
  68.9 0.9 slice_subtract_fusion.8
  69.9 0.1 fusion.7
  70.1 1.2 multiply_add_fusion.2
  71.3 5.5 %copy.52 = f32[5,8,16,256]{1,3,2,0:T(8,128)} copy(f32[5,8,16,256]{3,2,1,0:T(8,128)S(1)} %multiply_add_fusion.2) | data formatting | bytes 1310720 | tf_op jit(solution)/shard_map/add | solution.py:63
  76.8 14.6 %fusion.21 = (f32[5,8,8,1,128,1]{1,5,4,3,2,0:T(1,128)}, f32[5,8,8,1,128,1]{1,5,4,3,2,0:T(1,128)}, f32[5,8,8,1,128,1]{1,5,4,3,2,0:T(1,128)}, f32[5,8,8,1,128,1]{1,5,4,3,2,0:T(1,128)S(1)}) fusion(f32[5,8,8,2,128,2]{1,5,4,3,2,0:T(2,128)} %bitcast.27), kind=kLoop, calls=%fused_computation.83 | loop fusion | bytes 1310720 | tf_op jit(solution)/shard_map/slice | solution.py:75
  91.4 4.3 %copy.61 = f32[5,8,8,1,128,1]{4,2,1,0,5,3:T(8,128)} copy(f32[5,8,8,1,128,1]{1,5,4,3,2,0:T(1,128)} %get-tuple-element.9) | data formatting | bytes 327680
  95.7 4.3 %copy.62 = f32[5,8,8,1,128,1]{4,2,1,0,5,3:T(8,128)} copy(f32[5,8,8,1,128,1]{1,5,4,3,2,0:T(1,128)} %get-tuple-element.7) | data formatting | bytes 327680
  100.0 4.3 %copy.63 = f32[5,8,8,1,128,1]{4,2,1,0,5,3:T(8,128)} copy(f32[5,8,8,1,128,1]{1,5,4,3,2,0:T(1,128)} %get-tuple-element.8) | data formatting | bytes 327680
  104.4 2.5 %copy.64 = f32[5,8,8,1,128,1]{4,2,1,0,5,3:T(8,128)} copy(f32[5,8,8,1,128,1]{1,5,4,3,2,0:T(1,128)S(1)} %get-tuple-element.10) | data formatting | bytes 327680
  106.8 1.2 multiply_bitcast_fusion.filt
  108.1 2.2 %copy-done = f32[4,8,32,8,128]{4,3,2,1,0:T(8,128)S(1)} copy-done((f32[4,8,32,8,128]{4,3,2,1,0:T(8,128)S(1)}, f32[4,8,32,8,128]{4,3,2,1,0:T(8,128)}, u32[]{:S(2)}) %copy-start) | copy-done | bytes 4194328
  110.3 38.7 %shard_map.91 = bf16[8,32,8,128]{3,2,1,0:T(8,128)(2,1)S(1)} custom-call(f32[5,8,8,128]{3,2,1,0:T(8,128)S(1)} %multiply_bitcast_fusion.filt, f32[5,32]{1,0:T(8,128)S(1)} %copy-done.3, f32[32]{0:T(128)S(1)} %copy-done.4, bf16[256,256]{1,0:T(8,128)(2,1)S(1)} %mul.224.mixk, f32[256,1]{1,0:T(8,128)S(1)} %broadcast_in_dim_reshape.4.bias, ...), custom_call_target="tpu_custom_call" | custom-call | tf_op jit(solution)/shard_map/pallas_call | solution.py:326
  149.0 0.8 copy.78
  (39 shorter events, 0.4 us)
Async XLA Ops:
  0.0 5.9 %copy-start.6 = (f32[5,8,16,256]{3,2,1,0:T(8,128)S(1)}, f32[5,8,16,256]{3,2,1,0:T(8,128)}, u32[]{:S(2)}) copy-start(f32[5,8,16,256]{3,2,1,0:T(8,128)} %param.9) | copy-start | bytes 1966084
  0.0 6.9 %copy-start.7 = (bf16[32,32]{1,0:T(8,128)(2,1)S(1)}, bf16[32,32]{1,0:T(8,128)(2,1)}, u32[]{:S(2)}) copy-start(bf16[32,32]{1,0:T(8,128)(2,1)} %param.13) | copy-start | bytes 6148
  1.3 10.0 %collective-permute-start = (f32[6,8,3,256]{3,1,2,0:T(8,128)S(1)}, f32[6,8,3,256]{3,1,2,0:T(8,128)S(1)}, u32[]{:S(2)}, u32[]{:S(2)}) collective-permute-start(f32[6,8,3,256]{3,1,2,0:T(8,128)S(1)} %copy.59), channel_id=1, source_target_pairs={{0,8},{8,16},{16,24},{24,0},{1,9},{9,17},{17,25},{25,1},{2,10},{10... | collective-permute-start | bytes 442376 | tf_op jit(solution)/shard_map/ppermute | solution.py:30
  5.0 10.3 %collective-permute-start.1 = (f32[6,8,3,256]{3,1,2,0:T(8,128)}, f32[6,8,3,256]{3,1,2,0:T(8,128)S(1)}, u32[]{:S(2)}, u32[]{:S(2)}) collective-permute-start(f32[6,8,3,256]{3,1,2,0:T(8,128)} %copy.60), channel_id=1, source_target_pairs={{8,0},{16,8},{24,16},{0,24},{9,1},{17,9},{25,17},{1,25},{10,2},{18... | collective-permute-start | bytes 442376 | tf_op jit(solution)/shard_map/ppermute | solution.py:33
  20.5 8.2 %copy-start.8 = (f32[32]{0:T(128)S(1)}, f32[32]{0:T(128)}, u32[]{:S(2)}) copy-start(f32[32]{0:T(128)} %param.15) | copy-start | bytes 388
  20.5 8.4 %collective-permute-start.2 = (f32[6,8,22,3]{2,1,3,0:T(8,128)S(1)}, f32[6,8,22,3]{2,1,3,0:T(8,128)S(1)}, u32[]{:S(2)}, u32[]{:S(2)}) collective-permute-start(f32[6,8,22,3]{2,1,3,0:T(8,128)S(1)} %get-tuple-element.5), channel_id=1, source_target_pairs={{0,2},{2,4},{4,6},{6,0},{1,3},{3,5},{5,7},{7,1},{8,10},{10,12},{12... | collective-permute-start | bytes 38024 | tf_op jit(solution)/shard_map/ppermute | solution.py:30
  22.6 6.3 %collective-permute-start.3 = (f32[6,8,22,3]{2,1,3,0:T(8,128)S(1)}, f32[6,8,22,3]{2,1,3,0:T(8,128)S(1)}, u32[]{:S(2)}, u32[]{:S(2)}) collective-permute-start(f32[6,8,22,3]{2,1,3,0:T(8,128)S(1)} %get-tuple-element.6), channel_id=1, source_target_pairs={{2,0},{4,2},{6,4},{0,6},{3,1},{5,3},{7,5},{1,7},{10,8},{12,10},{14... | collective-permute-start | bytes 38024 | tf_op jit(solution)/shard_map/ppermute | solution.py:33
  37.1 3.7 %copy-start.5 = (f32[6,8,22,262]{2,1,3,0:T(8,128)}, f32[6,8,22,262]{2,1,3,0:T(8,128)S(1)}, u32[]{:S(2)}) copy-start(f32[6,8,22,262]{2,1,3,0:T(8,128)S(1)} %pad_maximum_fusion) | copy-start | bytes 3320068
  44.8 9.1 %collective-permute-start.4 = (f32[6,3,22,262]{3,2,1,0:T(8,128)}, f32[6,3,22,262]{3,2,1,0:T(8,128)}, u32[]{:S(2)}, u32[]{:S(2)}) collective-permute-start(f32[6,3,22,262]{3,2,1,0:T(8,128)} %copy.49), channel_id=1, source_target_pairs={{0,1},{1,0},{2,3},{3,2},{4,5},{5,4},{6,7},{7,6},{8,9},{9,8},{10,11... | collective-permute-start | bytes 1245032 | tf_op jit(solution)/shard_map/ppermute | solution.py:30
  47.1 6.8 %collective-permute-start.5 = (f32[6,3,22,262]{3,2,1,0:T(8,128)}, f32[6,3,22,262]{3,2,1,0:T(8,128)S(1)}, u32[]{:S(2)}, u32[]{:S(2)}) collective-permute-start(f32[6,3,22,262]{3,2,1,0:T(8,128)} %copy.50), channel_id=1, source_target_pairs={{1,0},{0,1},{3,2},{2,3},{5,4},{4,5},{7,6},{6,7},{9,8},{8,9},{11,10... | collective-permute-start | bytes 1245032 | tf_op jit(solution)/shard_map/ppermute | solution.py:33
  104.4 3.7 %copy-start.1 = (bf16[256,512]{1,0:T(8,128)(2,1)S(1)}, bf16[256,512]{1,0:T(8,128)(2,1)}, u32[]{:S(2)}) copy-start(bf16[256,512]{1,0:T(8,128)(2,1)} %constant.76.clone.x1) | copy-start | bytes 786436
  104.4 3.7 %copy-start.2 = (bf16[256,512]{1,0:T(8,128)(2,1)S(1)}, bf16[256,512]{1,0:T(8,128)(2,1)}, u32[]{:S(2)}) copy-start(bf16[256,512]{1,0:T(8,128)(2,1)} %constant.77.clone.x2) | copy-start | bytes 786436
  104.4 3.7 %copy-start.3 = (f32[5,32]{1,0:T(8,128)S(1)}, f32[5,32]{1,0:T(8,128)}, u32[]{:S(2)}) copy-start(f32[5,32]{1,0:T(8,128)} %lw.1) | copy-start | bytes 1924
  104.4 3.7 %copy-start.4 = (f32[32]{0:T(128)S(1)}, f32[32]{0:T(128)}, u32[]{:S(2)}) copy-start(f32[32]{0:T(128)} %lb.1) | copy-start | bytes 388
  108.1 2.2 %copy-start = (f32[4,8,32,8,128]{4,3,2,1,0:T(8,128)S(1)}, f32[4,8,32,8,128]{4,3,2,1,0:T(8,128)}, u32[]{:S(2)}) copy-start(f32[4,8,32,8,128]{4,3,2,1,0:T(8,128)} %w_hbm.1) | copy-start | bytes 12582916

commit v2 on v1

--- a/solution.py
+++ b/solution.py
@@ -21,72 +21,6 @@
 highest = lax.Precision.HIGHEST
 
 
-def padded_2(block, sides, width):
-    for axis, dim in sides:
-        count = lax.axis_size(axis)
-        forward = [(i, i + 1) for i in range(count - 1)]
-        forward.append((count - 1, 0))
-        backward = [(target, source) for source, target in forward]
-        low = lax.ppermute(
-            lax.slice_in_dim(block, block.shape[dim] - width, None, axis=dim), axis, forward
-        )
-        high = lax.ppermute(lax.slice_in_dim(block, 0, width, axis=dim), axis, backward)
-        block = jnp.concatenate([low, block, high], axis=dim)
-    return block
-
-
-def step_interior(padded, stiff_part):
-    center = padded[:, 1:-1, 1:-1, 1:-1]
-    upper_depth = padded[:, 2:, 1:-1, 1:-1]
-    lower_depth = padded[:, :-2, 1:-1, 1:-1]
-    upper_east = padded[:, 1:-1, 2:, 1:-1]
-    lower_east = padded[:, 1:-1, :-2, 1:-1]
-    upper_north = padded[:, 1:-1, 1:-1, 2:]
-    lower_north = padded[:, 1:-1, 1:-1, :-2]
-    slope_depth = upper_depth - lower_depth
-    slope_east = upper_east - lower_east
-    slope_north = upper_north - lower_north
-    curvature = (
-        upper_depth
-        + lower_depth
-        + upper_east
-        + lower_east
-        + upper_north
-        + lower_north
-        - 6.0 * center
-    )
-    transport = mean_flow[0] * slope_east + mean_flow[1] * slope_north + mean_flow[2] * slope_depth
-    diverge = slope_east[1] + slope_north[2] + slope_depth[3]
-    coupling = jnp.stack(
-        [diverge, slope_east[4], slope_north[4], slope_depth[4], stiff_part * diverge]
-    )
-    return center - courant_half * (transport + coupling) + smooth_half * curvature
-
-
-def trim(block, margin):
-    return block[margin:-margin, margin:-margin, margin:-margin]
-
-
-def coarsen(fields_now):
-    extent = fields_now.shape
-    blocks = fields_now.reshape(extent[0], extent[1], extent[2] // 2, 2, extent[3] // 2, 2)
-    return 0.25 * (
-        blocks[:, :, :, 0, :, 0]
-        + blocks[:, :, :, 1, :, 0]
-        + blocks[:, :, :, 0, :, 1]
-        + blocks[:, :, :, 1, :, 1]
-    )
-
-
-def angles(frequencies, points, length):
-    product = jnp.mod(frequencies[:, None] * points[None, :], length)
-    return product.astype(jnp.float32) * (2.0 * math.pi / length)
-
-
-def centered(number):
-    return jnp.arange(number, dtype=jnp.int32) - number // 2
-
-
 MESH = pl.DeviceIdType.MESH
 f32 = jnp.float32
 bf16 = jnp.bfloat16
@@ -125,32 +59,166 @@
     )
 
 
+def stencil_step(state, target, stiff, xr, yr, dims):
+    NZ, NX, NY = dims
+    eye = lax.broadcasted_iota(jnp.int32, (NZ * NX, NZ * NX), 0) == lax.broadcasted_iota(
+        jnp.int32, (NZ * NX, NZ * NX), 1
+    )
+    columns = [
+        [
+            jnp.sum(
+                jnp.where(eye, jnp.broadcast_to(yr[side, f : f + 1, :], eye.shape), 0.0),
+                axis=1,
+                keepdims=True,
+            )
+            for f in range(5)
+        ]
+        for side in range(2)
+    ]
+    row = lax.broadcasted_iota(jnp.int32, (NX, NY), 0)
+    lane = lax.broadcasted_iota(jnp.int32, (NX, NY), 1)
+    a, b = courant_half, smooth_half
+    for z in range(NZ):
+        near = []
+        for f in range(5):
+            c = state[f, z + 1]
+            span = slice(z * NX, (z + 1) * NX)
+            xl = jnp.where(row == 0, xr[0, f, z : z + 1, :], pltpu.roll(c, 1, 0))
+            xu = jnp.where(row == NX - 1, xr[1, f, z : z + 1, :], pltpu.roll(c, NX - 1, 0))
+            yl = jnp.where(lane == 0, columns[0][f][span], pltpu.roll(c, 1, 1))
+            yu = jnp.where(lane == NY - 1, columns[1][f][span], pltpu.roll(c, NY - 1, 1))
+            near.append((c, xl, xu, yl, yu, state[f, z], state[f, z + 2]))
+        diverge = (
+            (near[1][2] - near[1][1]) + (near[2][4] - near[2][3]) + (near[3][6] - near[3][5])
+        )
+        p = near[4]
+        coupling = (diverge, p[2] - p[1], p[4] - p[3], p[6] - p[5], stiff[z] * diverge)
+        for f in range(5):
+            c, xl, xu, yl, yu, zl, zu = near[f]
+            target[f, z + 1] = (
+                (1.0 - 6.0 * b) * c
+                + (b + a * mean_flow[0]) * xl
+                + (b - a * mean_flow[0]) * xu
+                + (b + a * mean_flow[1]) * yl
+                + (b - a * mean_flow[1]) * yu
+                + (b + a * mean_flow[2]) * zl
+                + (b - a * mean_flow[2]) * zu
+                - a * coupling[f]
+            )
+
+
 def layer_kernel(
     cfg,
-    filt, lw, lb, mixk, bias, base_e, base_d, cz, sz, x1, x2, w_hbm,
+    lw, lb, mix, bias_row, cz, sz, fields_hbm, stiff_hbm, ed_hbm, x1_hbm, x2_hbm, w_hbm,
     out,
+    state, stiff, xs, xr, ys, yr, pairs, filt, ed, x1, x2,
     lift, table, p_send, p_recv, p2, r2, q3, r3, c4, r4, rr, ii, mf, r5, r6, s7, r7, wv,
-    wsem, s1s, s1r, s2s, s2r, s3s, s3r, s4s, s4r, s5s, s5r, s6s, s6r, s7s, s7r,
+    local, hs, hr, s1s, s1r, s2s, s2r, s3s, s3r, s4s, s4r, s5s, s5r, s6s, s6r, s7s, s7r,
 ):
-    G, H, C, CB, KB, OB, KZ, NZL, XL, YL = cfg
+    G, H, A, C, CB, KB, OB, KZ, NZL, XL, YL = cfg
     Q = 2 * MY
+    NX, NY = 2 * XL, 2 * YL
     gx, gx_peers = peers("gx")
     gy, gy_peers = peers("gy")
     ga = lax.axis_index("ga")
-    other = 1 - ga
-    weights = pltpu.make_async_copy(w_hbm, wv, wsem)
-    weights.start()
+    other = lax.rem(ga + 1, A)
     barrier = pltpu.get_barrier_semaphore()
     for axis, group in (("gx", gx_peers), ("gy", gy_peers)):
         for _, peer, _ in group:
             pl.semaphore_signal(barrier, inc=1, device_id={axis: peer}, device_id_type=MESH)
     pl.semaphore_signal(barrier, inc=1, device_id={"ga": other}, device_id_type=MESH)
-
-    e, d = base_e[...], base_d[...]
-    for z in range(NZL):
-        for k in range(2 * KZ):
-            block = e * cz[z, k] + d * sz[z, k]
-            table[k // KZ, z * YL : (z + 1) * YL, (k % KZ) * Q : (k % KZ + 1) * Q] = block.astype(bf16)
+    loads = [
+        pltpu.make_async_copy(source, target, local.at[n])
+        for n, (source, target) in enumerate(
+            (
+                (fields_hbm, state.at[0, :, pl.ds(1, NZL)]),
+                (stiff_hbm, stiff),
+                (ed_hbm.at[gy], ed),
+                (x1_hbm, x1),
+                (x2_hbm, x2),
+                (w_hbm, wv),
+            )
+        )
+    ]
+    for load in loads:
+        load.start()
+
+    def build_table():
+        loads[2].wait()
+        e, d = ed[0], ed[1]
+        for z in range(NZL):
+            for k in range(2 * KZ):
+                at = ga * NZL + z
+                block = e * cz[at, k] + d * sz[at, k]
+                table[k // KZ, z * YL : (z + 1) * YL, (k % KZ) * Q : (k % KZ + 1) * Q] = block.astype(bf16)
+
+    loads[0].wait()
+    eye = lax.broadcasted_iota(jnp.int32, (NZL * NX, NZL * NX), 0) == lax.broadcasted_iota(
+        jnp.int32, (NZL * NX, NZL * NX), 1
+    )
+    for t in range(STEPS):
+        now = state.at[t]
+        for side, (edge_x, edge_y) in enumerate(((NX - 1, NY - 1), (0, 0))):
+            for f in range(5):
+                for z in range(NZL):
+                    xs[side, f, z : z + 1, :] = now[f, z + 1, edge_x : edge_x + 1, :]
+                column = now[f, 1 : NZL + 1, :, edge_y : edge_y + 1].reshape(NZL * NX, 1)
+                ys[side, f : f + 1, :] = jnp.sum(
+                    jnp.where(eye, jnp.broadcast_to(column, eye.shape), 0.0), axis=0, keepdims=True
+                )
+        if t == 0:
+            pl.semaphore_wait(barrier, (G - 1) + (H - 1) + 1)
+        copies = []
+        for side in range(2):
+            shift = 1 if side == 0 else -1
+            tx, ty, ta = (
+                lax.rem(lax.axis_index(n) + lax.axis_size(n) + shift, lax.axis_size(n))
+                for n in ("gx", "gy", "ga")
+            )
+            sems = (hs.at[t], hr.at[t])
+            copies.append(remote(ys.at[side], yr.at[t, side], sems, side, "gy", ty))
+            copies.append(remote(xs.at[side], xr.at[t, side], sems, 2 + side, "gx", tx))
+            plane, halo = (NZL, 0) if side == 0 else (1, NZL + 1)
+            copies.append(remote(now.at[:, plane], now.at[:, halo], sems, 4 + side, "ga", ta))
+        for one in copies:
+            one.start()
+        if t == 0:
+            build_table()
+            loads[1].wait()
+        for one in copies:
+            one.wait()
+        stencil_step(now, state.at[t + 1], stiff, xr.at[t], yr.at[t], (NZL, NX, NY))
+
+    both = lax.broadcasted_iota(jnp.int32, (NY, YL), 0) // 2 == lax.broadcasted_iota(
+        jnp.int32, (NY, YL), 1
+    )
+    both = jnp.where(both, 1.0, 0.0)
+    for f in range(5):
+        pairs[f] = lax.dot_general(
+            state[STEPS, f, 1 : NZL + 1].reshape(NZL * NX, NY),
+            both,
+            (((1,), (0,)), ((), ())),
+            precision=highest,
+            preferred_element_type=f32,
+        )
+        for z in range(NZL):
+            filt[f, z] = 0.25 * (
+                pairs[f, pl.ds(z * NX, XL, stride=2), :] + pairs[f, pl.ds(z * NX + 1, XL, stride=2), :]
+            )
+
+    spread = jnp.where(
+        lax.broadcasted_iota(jnp.int32, (C * XL, C), 0) // XL
+        == lax.broadcasted_iota(jnp.int32, (C * XL, C), 1),
+        1.0,
+        0.0,
+    )
+    bias = jnp.sum(spread * bias_row[...], axis=1, keepdims=True)
+    wide = dot(spread.astype(bf16), mix[...], ((1,), (1,))).astype(bf16)
+    wide = dot(wide, spread.astype(bf16), ((1,), (1,)))
+    same = lax.rem(lax.broadcasted_iota(jnp.int32, wide.shape, 0), XL) == lax.rem(
+        lax.broadcasted_iota(jnp.int32, wide.shape, 1), XL
+    )
+    mixk = jnp.where(same, wide, 0.0).astype(bf16)
 
     def lift_two(pair, carry):
         c = pair * 2
@@ -166,7 +234,6 @@
         return carry
 
     lax.fori_loop(0, C // 2, lift_two, 0)
-    pl.semaphore_wait(barrier, (G - 1) + (H - 1) + 1)
 
     p_send[...] = dot(lift[...], table[other]).astype(bf16)
     copy = remote(p_send, p_recv, (s1s, s1r), 0, "ga", other)
@@ -183,6 +250,7 @@
     r2[gx] = p2[gx]
     for one in copies:
         one.wait()
+    loads[3].wait()
     v = r2[...].reshape(C * XL, KZ * Q)
     vs = swapped(v.astype(f32)).astype(bf16)
     q3[...] = dot(x1[...], jnp.concatenate([v, vs], axis=0)).astype(bf16).reshape(q3.shape)
@@ -211,7 +279,7 @@
         turned = pltpu.roll(part, MY, 1)
         rr[k] = jnp.where(low, part, turned)
         ii[k] = jnp.where(low, turned, part)
-    weights.wait()
+    loads[5].wait()
 
     def mix_one(kx, carry):
         for k in range(KZ):
@@ -239,6 +307,8 @@
         forwards.append(remote(r5.at[source], r6.at[source], (s6s, s6r), n, "ga", other))
         forwards[-1].start()
 
+    loads[4].wait()
+
     def back(v):
         vs = swapped(v.astype(f32)).astype(bf16)
         return dot(x2[...], jnp.concatenate([v, vs], axis=0)).astype(bf16)
@@ -259,7 +329,7 @@
         copies.append(remote(s7.at[peer], r7.at[gx], (s7s, s7r), n - 1, "gx", peer))
         copies[-1].start()
     r7[gx] = s7[gx]
-    direct = dot(mixk[...], lift[...]) + bias[...]
+    direct = dot(mixk, lift[...]) + bias
     for one in copies:
         one.wait()
     for z in range(NZL):
@@ -293,30 +363,27 @@
     return jnp.asarray(x1, bf16), jnp.asarray(x2, bf16)
 
 
+def north_tables(H, YL, NZ):
+    length = H * YL
+    n = np.arange(MY) - MY // 2
+    u = 2.0 * np.pi * ((np.arange(length)[:, None] * n[None, :]) % length) / length
+    scale = 1.0 / math.sqrt(length * NZ)
+    cu, su = np.cos(u) * scale, np.sin(u) * scale
+    both = np.stack([np.concatenate([cu, -su], axis=1), np.concatenate([-su, -cu], axis=1)])
+    return jnp.asarray(both.reshape(2, H, YL, 2 * MY).transpose(1, 0, 2, 3), f32)
+
+
 def shards(fields, stiffness, lift_weight, lift_bias, mix_weight, spectral_weight, output_bias):
     G, H, A = (lax.axis_size(n) for n in ("gx", "gy", "ga"))
-    stacked = jnp.concatenate([fields, stiffness[None]], axis=0)
-    padded = padded_2(stacked, (("gx", 2), ("gy", 3), ("ga", 1)), STEPS)
-    fields_now = padded[:5]
-    for repeat in range(STEPS):
-        fields_now = step_interior(fields_now, trim(padded[5], repeat + 1))
-    filtered = coarsen(fields_now)
-    _, NZL, XL, YL = filtered.shape
+    _, NZL, NX, NY = fields.shape
+    XL, YL = NX // 2, NY // 2
     C = lift_weight.shape[1]
     CB, KB, OB, KZ, Q = C // G, MX // H, C // G, MZ // A, 2 * MY
-    length_z, length_y = NZL * A, YL * H
-    y_points = lax.axis_index("gy") * YL + jnp.arange(YL, dtype=jnp.int32)
-    u = angles(centered(MY), y_points, length_y).T
-    scale = 1.0 / math.sqrt(length_y * length_z)
-    cu, su = jnp.cos(u) * scale, jnp.sin(u) * scale
-    base_e = jnp.concatenate([cu, -su], axis=1)
-    base_d = jnp.concatenate([-su, -cu], axis=1)
-    z_points = lax.axis_index("ga") * NZL + jnp.arange(NZL, dtype=jnp.int32)
-    v = angles(jnp.arange(MZ, dtype=jnp.int32), z_points, length_z).T
+    NZ = NZL * A
+    v = 2.0 * np.pi * ((np.arange(NZ)[:, None] * np.arange(MZ)[None, :]) % NZ) / NZ
     x1, x2 = east_tables(G, H, XL, C)
-    mixk = jnp.kron(mix_weight.T, jnp.eye(XL, dtype=bf16))
-    bias = jnp.repeat(output_bias, XL)[:, None]
-    cfg = (G, H, C, CB, KB, OB, KZ, NZL, XL, YL)
+    ed = north_tables(H, YL, NZ)
+    cfg = (G, H, A, C, CB, KB, OB, KZ, NZL, XL, YL)
     vmem = pl.BlockSpec(memory_space=pltpu.VMEM)
     smem = pl.BlockSpec(memory_space=pltpu.SMEM)
     hbm = pl.BlockSpec(memory_space=pl.ANY)
@@ -326,9 +393,20 @@
     return pl.pallas_call(
         functools.partial(layer_kernel, cfg),
         out_shape=jax.ShapeDtypeStruct((NZL, C, XL, YL), bf16),
-        in_specs=[vmem, smem, smem, vmem, vmem, vmem, vmem, smem, smem, vmem, vmem, hbm],
+        in_specs=[smem, smem, vmem, vmem, smem, smem, hbm, hbm, hbm, hbm, hbm, hbm],
         out_specs=vmem,
         scratch_shapes=[
+            V((STEPS + 1, 5, NZL + 2, NX, NY), f32),
+            V((NZL, NX, NY), f32),
+            V((2, 5, NZL, NY), f32),
+            V((STEPS, 2, 5, NZL, NY), f32),
+            V((2, 5, NZL * NX), f32),
+            V((STEPS, 2, 5, NZL * NX), f32),
+            V((5, NZL * NX, YL), f32),
+            V((5, NZL, XL, YL), f32),
+            V(ed.shape[1:], f32),
+            V(x1.shape, bf16),
+            V(x2.shape, bf16),
             V((C * XL, NZL * YL), bf16),
             V((A, NZL * YL, L), bf16),
             V((C * XL, L), bf16),
@@ -347,7 +425,8 @@
             V((G, OB * XL, NZL * YL), bf16),
             V((G, OB * XL, NZL * YL), bf16),
             V(spectral_weight.shape, f32),
-            dma,
+            dma((6,)),
+            dma((STEPS, 6)), dma((STEPS, 6)),
             dma((1,)), dma((1,)),
             dma((G - 1,)), dma((G - 1,)),
             dma((H - 1,)), dma((H - 1,)),
@@ -358,8 +437,9 @@
         ],
         compiler_params=pltpu.CompilerParams(collective_id=0, has_side_effects=True, vmem_limit_bytes=48 * 2**20),
     )(
-        filtered, lift_weight, lift_bias, mixk, bias, base_e, base_d,
-        jnp.cos(v), jnp.sin(v), x1, x2, spectral_weight,
+        lift_weight, lift_bias, mix_weight, output_bias[None, :],
+        jnp.asarray(np.cos(v), f32), jnp.asarray(np.sin(v), f32),
+        fields, stiffness, ed, x1, x2, spectral_weight,
     )
 
 

time: 151 us -> 69.9 us (0.46)
  local copies, waits for them, and re-layouts: 69.8 us -> 9.81 us
  other arithmetic: 32 us -> 0 us
  Pallas kernels: 38.7 us -> 59.6 us
  starting transfers between devices: 8.86 us -> 0 us
    slice x4 -> x0, local copies, waits for them, and re-layouts: 24.1 us -> none  [the longest x1 14.6 us: coarsen(): blocks[:, :, :, 1, :, 0]]
    pallas_call x1, Pallas kernels: 38.7 us -> 59.6 us  [shards(): pl.pallas_call(functools.partial(layer_kernel, cfg), out_shape=jax.ShapeD...]
    concatenate x5 -> x0, other arithmetic: 12.7 us -> none  [the longest x2 9.48 us: padded_2(): block = jnp.concatenate([low, block, high], axis=dim)]
    unnamed x34 -> x23, local copies, waits for them, and re-layouts: 19.9 us -> 9.81 us
    concatenate x2 -> x0, local copies, waits for them, and re-layouts: 9.13 us -> none  [the longest x1 5.11 us: padded_2(): block = jnp.concatenate([low, block, high], axis=dim)]
    ppermute x6 -> x0, starting transfers between devices: 8.86 us -> none  [the longest x3 5.11 us: padded_2(): lax.ppermute(lax.slice_in_dim(block, block.shape[dim] - width, None, axis...]
    add x5 -> x0, other arithmetic: 8.57 us -> none  [the longest x3 8.56 us: step_interior(): center - courant_half * (transport + coupling) + smooth_half * curvature]
    ppermute x2 -> x0, local copies, waits for them, and re-layouts: 7.98 us -> none  [the longest x1 4 us: padded_2(): lax.ppermute(lax.slice_in_dim(block, 0, width, axis=dim), axis, backward)]
  transfers between devices with their start and end apart: 6 -> 0, of which waited for: 0 -> 0; matrix products, arithmetic and copies ran while one was open for 15% -> 0% of each run, Pallas kernels for 0% -> 0%
where the time goes in v2:
time: 69.9 us; the launch traced here: 69.4 us
  Pallas kernels  59.6 us (85%)
  local copies, waits for them, and re-layouts  9.81 us (14%)
    pallas_call x1, Pallas kernels, shards(): pl.pallas_call(functools.partial(layer_kernel, cfg), out_shape=jax.ShapeD...  59.6 us
    unnamed x23, local copies, waits for them, and re-layouts  9.81 us

profile of v2, /device:TPU:0, one launch (start us, length us, event | category | flops | bytes accessed | tf_op | source)
XLA Modules:
  0.0 69.4 jit_solution(13042774809114272127)
XLA Ops:
  0.0 0.0 copy-start
  0.0 1.1 %copy-done = f32[5,8,16,256]{3,2,1,0:T(8,128)S(1)} copy-done((f32[5,8,16,256]{3,2,1,0:T(8,128)S(1)}, f32[5,8,16,256]{3,2,1,0:T(8,128)}, u32[]{:S(2)}) %copy-start) | copy-done | bytes 655384
  1.1 0.0 copy-start.1
  1.1 1.0 %copy-done.1 = f32[4,2,128,128]{3,2,1,0:T(8,128)S(1)} copy-done((f32[4,2,128,128]{3,2,1,0:T(8,128)S(1)}, f32[4,2,128,128]{3,2,1,0:T(8,128)}, u32[]{:S(2)}) %copy-start.1) | copy-done | bytes 524312
  2.1 0.0 copy-start.2
  2.1 0.9 %copy-done.2 = bf16[256,512]{1,0:T(8,128)(2,1)S(1)} copy-done((bf16[256,512]{1,0:T(8,128)(2,1)S(1)}, bf16[256,512]{1,0:T(8,128)(2,1)}, u32[]{:S(2)}) %copy-start.2) | copy-done | bytes 262168
  3.1 0.0 copy-start.3
  3.1 0.9 %copy-done.3 = bf16[256,512]{1,0:T(8,128)(2,1)S(1)} copy-done((bf16[256,512]{1,0:T(8,128)(2,1)S(1)}, bf16[256,512]{1,0:T(8,128)(2,1)}, u32[]{:S(2)}) %copy-start.3) | copy-done | bytes 262168
  4.0 0.0 copy-start.4
  4.0 0.9 %copy-done.4 = f32[8,16,256]{2,1,0:T(8,128)S(1)} copy-done((f32[8,16,256]{2,1,0:T(8,128)S(1)}, f32[8,16,256]{2,1,0:T(8,128)}, u32[]{:S(2)}) %copy-start.4) | copy-done | bytes 131096
  4.9 0.0 copy-start.5
  4.9 0.7 %copy-done.5 = bf16[32,32]{1,0:T(8,128)(2,1)S(1)} copy-done((bf16[32,32]{1,0:T(8,128)(2,1)S(1)}, bf16[32,32]{1,0:T(8,128)(2,1)}, u32[]{:S(2)}) %copy-start.5) | copy-done | bytes 2072
  5.6 0.0 copy-start.6
  5.6 0.7 %copy-done.6 = f32[16,8]{1,0:T(8,128)S(1)} copy-done((f32[16,8]{1,0:T(8,128)S(1)}, f32[16,8]{1,0:T(8,128)}, u32[]{:S(2)}) %copy-start.6) | copy-done | bytes 536
  6.3 0.0 copy-start.7
  6.3 0.7 %copy-done.7 = f32[16,8]{1,0:T(8,128)S(1)} copy-done((f32[16,8]{1,0:T(8,128)S(1)}, f32[16,8]{1,0:T(8,128)}, u32[]{:S(2)}) %copy-start.7) | copy-done | bytes 536
  7.0 0.0 copy-start.8
  7.0 0.7 copy-done.8
  7.7 0.0 copy-start.9
  7.7 0.7 copy-done.9
  8.4 0.0 copy-start.10
  8.4 0.7 copy-done.10
  9.0 59.6 %shard_map.118 = bf16[8,32,8,128]{3,2,1,0:T(8,128)(2,1)S(1)} custom-call(f32[5,32]{1,0:T(8,128)S(1)} %copy-done.8, f32[32]{0:T(128)S(1)} %copy-done.9, bf16[32,32]{1,0:T(8,128)(2,1)S(1)} %copy-done.5, f32[1,32]{1,0:T(1,128)S(1)} %bitcast.1, f32[16,8]{1,0:T(8,128)S(1)} %copy-done.7, f32[16,8]{1,0:T(8,128)S(1)} %copy-done.6, f32[5,8,16,256]{3,2,1,0:T(8,128)S(1)} %copy-done, ...), custom_call_target="tpu_custom_call" | custom-call | tf_op jit(solution)/shard_map/pallas_call | solution.py:393
  68.6 0.8 %copy.14 = bf16[8,32,8,128]{3,2,1,0:T(8,128)(2,1)} copy(bf16[8,32,8,128]{3,2,1,0:T(8,128)(2,1)S(1)} %shard_map.118) | data formatting | bytes 1048576
Async XLA Ops:
  0.0 1.1 %copy-start = (f32[5,8,16,256]{3,2,1,0:T(8,128)S(1)}, f32[5,8,16,256]{3,2,1,0:T(8,128)}, u32[]{:S(2)}) copy-start(f32[5,8,16,256]{3,2,1,0:T(8,128)} %fields_hbm.1) | copy-start | bytes 1966084
  1.1 1.0 %copy-start.1 = (f32[4,2,128,128]{3,2,1,0:T(8,128)S(1)}, f32[4,2,128,128]{3,2,1,0:T(8,128)}, u32[]{:S(2)}) copy-start(f32[4,2,128,128]{3,2,1,0:T(8,128)} %constant.12.clone.ed_hbm) | copy-start | bytes 1572868
  2.1 0.9 %copy-start.2 = (bf16[256,512]{1,0:T(8,128)(2,1)S(1)}, bf16[256,512]{1,0:T(8,128)(2,1)}, u32[]{:S(2)}) copy-start(bf16[256,512]{1,0:T(8,128)(2,1)} %constant.11.clone.x2_hbm) | copy-start | bytes 786436
  3.1 0.9 %copy-start.3 = (bf16[256,512]{1,0:T(8,128)(2,1)S(1)}, bf16[256,512]{1,0:T(8,128)(2,1)}, u32[]{:S(2)}) copy-start(bf16[256,512]{1,0:T(8,128)(2,1)} %constant.10.clone.x1_hbm) | copy-start | bytes 786436
  4.0 0.9 %copy-start.4 = (f32[8,16,256]{2,1,0:T(8,128)S(1)}, f32[8,16,256]{2,1,0:T(8,128)}, u32[]{:S(2)}) copy-start(f32[8,16,256]{2,1,0:T(8,128)} %stiff_hbm.1) | copy-start | bytes 393220
  4.9 0.7 %copy-start.5 = (bf16[32,32]{1,0:T(8,128)(2,1)S(1)}, bf16[32,32]{1,0:T(8,128)(2,1)}, u32[]{:S(2)}) copy-start(bf16[32,32]{1,0:T(8,128)(2,1)} %mix.1) | copy-start | bytes 6148
  5.6 0.7 %copy-start.6 = (f32[16,8]{1,0:T(8,128)S(1)}, f32[16,8]{1,0:T(8,128)}, u32[]{:S(2)}) copy-start(f32[16,8]{1,0:T(8,128)} %constant.14.clone.sz) | copy-start | bytes 1540
  6.3 0.7 %copy-start.7 = (f32[16,8]{1,0:T(8,128)S(1)}, f32[16,8]{1,0:T(8,128)}, u32[]{:S(2)}) copy-start(f32[16,8]{1,0:T(8,128)} %constant.13.clone.cz) | copy-start | bytes 1540
  7.0 0.7 copy-start.8
  7.7 0.7 copy-start.9
  8.4 0.7 copy-start.10

commit v3 on v2

--- a/solution.py
+++ b/solution.py
@@ -13,6 +13,8 @@
 MX = 32
 MY = 64
 MZ = 8
+MODE_CHUNKS = 2
+DEPTH_CHUNKS = 4
 
 
 courant_half = 0.1
@@ -109,10 +111,10 @@
 
 def layer_kernel(
     cfg,
-    lw, lb, mix, bias_row, cz, sz, fields_hbm, stiff_hbm, ed_hbm, x1_hbm, x2_hbm, w_hbm,
+    fields_hbm, stiff_hbm, ed_hbm, x1_hbm, x2_hbm, w_hbm, lw_hbm, lb_hbm, mix_hbm, bias_hbm,
     out,
-    state, stiff, xs, xr, ys, yr, pairs, filt, ed, x1, x2,
-    lift, table, p_send, p_recv, p2, r2, q3, r3, c4, r4, rr, ii, mf, r5, r6, s7, r7, wv,
+    state, stiff, xs, xr, ys, yr, pairs, filt, ed, x1, x2, wv, lw, lb, mix, bias_row, wide_lift,
+    lift, table, p_send, p_recv, p2, r2, q3, r3, c4, r4, rr, ii, mf, r5, r6, s7, r7,
     local, hs, hr, s1s, s1r, s2s, s2r, s3s, s3r, s4s, s4r, s5s, s5r, s6s, s6r, s7s, s7r,
 ):
     G, H, A, C, CB, KB, OB, KZ, NZL, XL, YL = cfg
@@ -137,20 +139,53 @@
                 (x1_hbm, x1),
                 (x2_hbm, x2),
                 (w_hbm, wv),
+                (lw_hbm, lw),
+                (lb_hbm, lb),
+                (mix_hbm, mix),
+                (bias_hbm, bias_row),
             )
         )
     ]
     for load in loads:
         load.start()
 
+    NCH, NZC = MODE_CHUNKS, DEPTH_CHUNKS
+    KC = KZ // NCH
+    W = KC * Q
+    ZC = NZL // NZC
+    NZ = NZL * A
+
+    def own(values):
+        picked = jnp.float32(values[0])
+        for n in range(1, A):
+            picked = jnp.where(ga == n, jnp.float32(values[n]), picked)
+        return picked
+
     def build_table():
         loads[2].wait()
         e, d = ed[0], ed[1]
         for z in range(NZL):
-            for k in range(2 * KZ):
-                at = ga * NZL + z
-                block = e * cz[at, k] + d * sz[at, k]
-                table[k // KZ, z * YL : (z + 1) * YL, (k % KZ) * Q : (k % KZ + 1) * Q] = block.astype(bf16)
+            for k in range(A * KZ):
+                v = [2.0 * math.pi * ((k * (n * NZL + z)) % NZ) / NZ for n in range(A)]
+                block = e * own([math.cos(x) for x in v]) + d * own([math.sin(x) for x in v])
+                table[k // KC, z * YL : (z + 1) * YL, (k % KC) * Q : (k % KC + 1) * Q] = block.astype(bf16)
+
+    spread = jnp.where(
+        lax.broadcasted_iota(jnp.int32, (C * XL, C), 0) // XL
+        == lax.broadcasted_iota(jnp.int32, (C * XL, C), 1),
+        1.0,
+        0.0,
+    )
+
+    def tall(values):
+        return jnp.sum(spread * values, axis=1, keepdims=True)
+
+    def build_lift():
+        for n in (6, 7):
+            loads[n].wait()
+        for f in range(6):
+            values = lw[f : f + 1, :] if f < 5 else lb[...]
+            wide_lift[f] = jnp.broadcast_to(tall(values), (C * XL, YL))
 
     loads[0].wait()
     eye = lax.broadcasted_iota(jnp.int32, (NZL * NX, NZL * NX), 0) == lax.broadcasted_iota(
@@ -185,6 +220,8 @@
         if t == 0:
             build_table()
             loads[1].wait()
+        if t == STEPS - 1:
+            build_lift()
         for one in copies:
             one.wait()
         stencil_step(now, state.at[t + 1], stiff, xr.at[t], yr.at[t], (NZL, NX, NY))
@@ -206,13 +243,106 @@
                 pairs[f, pl.ds(z * NX, XL, stride=2), :] + pairs[f, pl.ds(z * NX + 1, XL, stride=2), :]
             )
 
-    spread = jnp.where(
-        lax.broadcasted_iota(jnp.int32, (C * XL, C), 0) // XL
-        == lax.broadcasted_iota(jnp.int32, (C * XL, C), 1),
-        1.0,
-        0.0,
-    )
-    bias = jnp.sum(spread * bias_row[...], axis=1, keepdims=True)
+    def lift_two(pair, carry):
+        rows = pl.ds(pl.multiple_of(pair * 2 * XL, 2 * XL), 2 * XL)
+        weights = [wide_lift[f, rows, :] for f in range(6)]
+        for z in range(NZL):
+            v = weights[5]
+            for f in range(5):
+                v = v + jnp.concatenate([filt[f, z], filt[f, z]], axis=0) * weights[f]
+            lift[rows, z * YL : (z + 1) * YL] = gelu(v).astype(bf16)
+        return carry
+
+    lax.fori_loop(0, C // 2, lift_two, 0)
+
+    stage1 = []
+    for h in range(NCH):
+        p_send[h] = dot(lift[...], table[other * NCH + h]).astype(bf16)
+        stage1.append(remote(p_send.at[h], p_recv.at[h], (s1s, s1r), h, "ga", other))
+        stage1[-1].start()
+
+    stage2 = []
+    for h in range(NCH):
+        mine = dot(lift[...], table[ga * NCH + h])
+        stage1[h].wait()
+        p2[h] = (mine + p_recv[h].astype(f32)).astype(bf16).reshape(p2.shape[1:])
+        group = []
+        for n, peer, _ in gx_peers:
+            slot = h * (G - 1) + n - 1
+            group.append(remote(p2.at[h, peer], r2.at[h, gx], (s2s, s2r), slot, "gx", peer))
+            group[-1].start()
+        r2[h, gx] = p2[h, gx]
+        stage2.append(group)
+
+    loads[3].wait()
+    stage3 = []
+    for h in range(NCH):
+        for one in stage2[h]:
+            one.wait()
+        v = r2[h].reshape(C * XL, W)
+        vs = swapped(v.astype(f32)).astype(bf16)
+        q3[h] = dot(x1[...], jnp.concatenate([v, vs], axis=0)).astype(bf16).reshape(q3.shape[1:])
+        group = []
+        for n, peer, _ in gy_peers:
+            slot = h * (H - 1) + n - 1
+            group.append(remote(q3.at[h, peer], r3.at[h, n - 1], (s3s, s3r), slot, "gy", peer))
+            group[-1].start()
+        stage3.append(group)
+
+    stage4 = []
+    for h in range(NCH):
+        acc = q3[h, gy].astype(f32)
+        for n, one in enumerate(stage3[h]):
+            one.wait()
+            acc = acc + r3[h, n].astype(f32)
+        c4[h] = acc.astype(bf16)
+        group = []
+        for n, peer, _ in gx_peers:
+            slot = h * (G - 1) + n - 1
+            group.append(remote(c4.at[h], r4.at[h, gx], (s4s, s4r), slot, "gx", peer))
+            group[-1].start()
+        r4[h, gx] = c4[h]
+        stage4.append(group)
+
+    loads[5].wait()
+    low = lax.broadcasted_iota(jnp.int32, (C * KB, Q), 1) < MY
+    stage5 = []
+    stage6 = []
+    for h in range(NCH):
+        for one in stage4[h]:
+            one.wait()
+        v = r4[h].reshape(C * KB, W).astype(f32)
+        for k in range(KC):
+            part = v[:, k * Q : (k + 1) * Q]
+            turned = pltpu.roll(part, MY, 1)
+            rr[h * KC + k] = jnp.where(low, part, turned)
+            ii[h * KC + k] = jnp.where(low, turned, part)
+
+        def mix_one(kx, carry):
+            for k in range(KC):
+                a = jnp.zeros((OB, Q), f32)
+                b = jnp.zeros((OB, Q), f32)
+                for c in range(C):
+                    w = wv[h * KC + k, kx, c]
+                    a = a + w * rr[h * KC + k, pl.ds(c * KB + kx, 1), :]
+                    b = b + w * ii[h * KC + k, pl.ds(c * KB + kx, 1), :]
+                mf[h, kx, :, k * Q : (k + 1) * Q] = a - swapped(b)
+            return carry
+
+        lax.fori_loop(0, KB, mix_one, 0)
+        r5[h, gy] = mf[h].reshape(KB * OB, W).astype(bf16)
+        group = []
+        for n, peer, _ in gy_peers:
+            slot = h * (H - 1) + n - 1
+            group.append(remote(r5.at[h, gy], r5.at[h, gy], (s5s, s5r), slot, "gy", peer))
+            group[-1].start()
+        stage5.append(group)
+        stage6.append([remote(r5.at[h, gy], r6.at[h, gy], (s6s, s6r), h * H, "ga", other)])
+        stage6[h][0].start()
+
+    loads[8].wait()
+    loads[9].wait()
+    bias = tall(bias_row[...])
     wide = dot(spread.astype(bf16), mix[...], ((1,), (1,))).astype(bf16)
     wide = dot(wide, spread.astype(bf16), ((1,), (1,)))
     same = lax.rem(lax.broadcasted_iota(jnp.int32, wide.shape, 0), XL) == lax.rem(
@@ -220,122 +350,52 @@
     )
     mixk = jnp.where(same, wide, 0.0).astype(bf16)
 
-    def lift_two(pair, carry):
-        c = pair * 2
-        rows = pl.ds(pl.multiple_of(pair * 2 * XL, 2 * XL), 2 * XL)
-        for z in range(NZL):
-            halves = []
-            for h in range(2):
-                v = filt[0, z] * lw[0, c + h]
-                for f in range(1, 5):
-                    v = v + filt[f, z] * lw[f, c + h]
-                halves.append(gelu(v + lb[c + h]))
-            lift[rows, z * YL : (z + 1) * YL] = jnp.concatenate(halves, axis=0).astype(bf16)
-        return carry
-
-    lax.fori_loop(0, C // 2, lift_two, 0)
-
-    p_send[...] = dot(lift[...], table[other]).astype(bf16)
-    copy = remote(p_send, p_recv, (s1s, s1r), 0, "ga", other)
-    copy.start()
-    mine = dot(lift[...], table[ga])
-    copy.wait()
-    total = (mine + p_recv[...].astype(f32)).astype(bf16)
-    p2[...] = total.reshape(p2.shape)
-
-    copies = []
-    for n, peer, _ in gx_peers:
-        copies.append(remote(p2.at[peer], r2.at[gx], (s2s, s2r), n - 1, "gx", peer))
-        copies[-1].start()
-    r2[gx] = p2[gx]
-    for one in copies:
-        one.wait()
-    loads[3].wait()
-    v = r2[...].reshape(C * XL, KZ * Q)
-    vs = swapped(v.astype(f32)).astype(bf16)
-    q3[...] = dot(x1[...], jnp.concatenate([v, vs], axis=0)).astype(bf16).reshape(q3.shape)
-
-    copies = []
-    for n, peer, _ in gy_peers:
-        copies.append(remote(q3.at[peer], r3.at[n - 1], (s3s, s3r), n - 1, "gy", peer))
-        copies[-1].start()
-    acc = q3[gy].astype(f32)
-    for n, one in enumerate(copies):
-        one.wait()
-        acc = acc + r3[n].astype(f32)
-    c4[...] = acc.astype(bf16)
-
-    copies = []
-    for n, peer, _ in gx_peers:
-        copies.append(remote(c4, r4.at[gx], (s4s, s4r), n - 1, "gx", peer))
-        copies[-1].start()
-    r4[gx] = c4[...]
-    for one in copies:
-        one.wait()
-    v = r4[...].reshape(C * KB, KZ * Q).astype(f32)
-    low = lax.broadcasted_iota(jnp.int32, (C * KB, Q), 1) < MY
-    for k in range(KZ):
-        part = v[:, k * Q : (k + 1) * Q]
-        turned = pltpu.roll(part, MY, 1)
-        rr[k] = jnp.where(low, part, turned)
-        ii[k] = jnp.where(low, turned, part)
-    loads[5].wait()
-
-    def mix_one(kx, carry):
-        for k in range(KZ):
-            lanes = slice(k * Q, (k + 1) * Q)
-            a = jnp.zeros((OB, Q), f32)
-            b = jnp.zeros((OB, Q), f32)
-            for c in range(C):
-                w = wv[k, kx, c]
-                a = a + w * rr[k, pl.ds(c * KB + kx, 1), :]
-                b = b + w * ii[k, pl.ds(c * KB + kx, 1), :]
-            mf[kx, :, lanes] = a - swapped(b)
-        return carry
-
-    lax.fori_loop(0, KB, mix_one, 0)
-
-    r5[gy] = mf[...].reshape(KB * OB, KZ * Q).astype(bf16)
-    copies = []
-    for n, peer, _ in gy_peers:
-        copies.append(remote(r5.at[gy], r5.at[gy], (s5s, s5r), n - 1, "gy", peer))
-        copies[-1].start()
-    forwards = [remote(r5.at[gy], r6.at[gy], (s6s, s6r), 0, "ga", other)]
-    forwards[0].start()
-    for (n, _, source), one in zip(gy_peers, copies):
-        one.wait_recv()
-        forwards.append(remote(r5.at[source], r6.at[source], (s6s, s6r), n, "ga", other))
-        forwards[-1].start()
-
     loads[4].wait()
+    rows = H * KB * OB
 
     def back(v):
+        v = v.reshape(rows, W)
         vs = swapped(v.astype(f32)).astype(bf16)
         return dot(x2[...], jnp.concatenate([v, vs], axis=0)).astype(bf16)
 
-    rows = H * KB * OB
-    y_mine = back(r5[...].reshape(rows, KZ * Q))
-    spec = dot(y_mine, table[ga], ((1,), (1,)))
-    for one in copies:
-        one.wait_send()
-    for one in forwards:
-        one.wait()
-    y_other = back(r6[...].reshape(rows, KZ * Q))
-    spec = spec + dot(y_other, table[other], ((1,), (1,)))
-    s7[...] = spec.astype(bf16).reshape(s7.shape)
-
-    copies = []
-    for n, peer, _ in gx_peers:
-        copies.append(remote(s7.at[peer], r7.at[gx], (s7s, s7r), n - 1, "gx", peer))
-        copies[-1].start()
-    r7[gx] = s7[gx]
-    direct = dot(mixk, lift[...]) + bias
-    for one in copies:
-        one.wait()
-    for z in range(NZL):
-        lanes = slice(z * YL, (z + 1) * YL)
-        both = direct[:, lanes] + r7[:, :, lanes].reshape(C * XL, YL).astype(f32)
-        out[z] = gelu(both).astype(bf16).reshape(C, XL, YL)
+    modes = []
+    for h in range(NCH):
+        for (n, _, source), one in zip(gy_peers, stage5[h]):
+            one.wait_recv()
+            stage6[h].append(
+                remote(r5.at[h, source], r6.at[h, source], (s6s, s6r), h * H + n, "ga", other)
+            )
+            stage6[h][-1].start()
+        modes.append((ga * NCH + h, back(r5[h])))
+    for h in range(NCH):
+        for one in stage5[h]:
+            one.wait_send()
+        for one in stage6[h]:
+            one.wait()
+        modes.append((other * NCH + h, back(r6[h])))
+
+    stage7 = []
+    for j in range(NZC):
+        span = slice(j * ZC * YL, (j + 1) * ZC * YL)
+        spec = dot(modes[0][1], table[modes[0][0], span, :], ((1,), (1,)))
+        for at, y in modes[1:]:
+            spec = spec + dot(y, table[at, span, :], ((1,), (1,)))
+        s7[j] = spec.astype(bf16).reshape(s7.shape[1:])
+        group = []
+        for n, peer, _ in gx_peers:
+            slot = j * (G - 1) + n - 1
+            group.append(remote(s7.at[j, peer], r7.at[j, gx], (s7s, s7r), slot, "gx", peer))
+            group[-1].start()
+        r7[j, gx] = s7[j, gx]
+        stage7.append(group)
+    for j in range(NZC):
+        span = slice(j * ZC * YL, (j + 1) * ZC * YL)
+        direct = dot(mixk, lift[:, span]) + bias
+        for one in stage7[j]:
+            one.wait()
+        both = gelu(direct + r7[j].reshape(C * XL, ZC * YL).astype(f32)).astype(bf16)
+        for z in range(ZC):
+            out[j * ZC + z] = both[:, z * YL : (z + 1) * YL].reshape(C, XL, YL)
 
 
 def east_tables(G, H, XL, C):
@@ -380,20 +440,20 @@
     C = lift_weight.shape[1]
     CB, KB, OB, KZ, Q = C // G, MX // H, C // G, MZ // A, 2 * MY
     NZ = NZL * A
-    v = 2.0 * np.pi * ((np.arange(NZ)[:, None] * np.arange(MZ)[None, :]) % NZ) / NZ
     x1, x2 = east_tables(G, H, XL, C)
     ed = north_tables(H, YL, NZ)
     cfg = (G, H, A, C, CB, KB, OB, KZ, NZL, XL, YL)
     vmem = pl.BlockSpec(memory_space=pltpu.VMEM)
-    smem = pl.BlockSpec(memory_space=pltpu.SMEM)
-    hbm = pl.BlockSpec(memory_space=pl.ANY)
-    L = KZ * Q
+    hbm = pl.BlockSpec(memory_space=pltpu.HBM)
+    NCH, NZC = MODE_CHUNKS, DEPTH_CHUNKS
+    W = KZ // NCH * Q
+    ZW = NZL // NZC * YL
     dma = pltpu.SemaphoreType.DMA
     V = pltpu.VMEM
     return pl.pallas_call(
         functools.partial(layer_kernel, cfg),
         out_shape=jax.ShapeDtypeStruct((NZL, C, XL, YL), bf16),
-        in_specs=[smem, smem, vmem, vmem, smem, smem, hbm, hbm, hbm, hbm, hbm, hbm],
+        in_specs=[hbm] * 10,
         out_specs=vmem,
         scratch_shapes=[
             V((STEPS + 1, 5, NZL + 2, NX, NY), f32),
@@ -407,39 +467,43 @@
             V(ed.shape[1:], f32),
             V(x1.shape, bf16),
             V(x2.shape, bf16),
+            V(spectral_weight.shape, f32),
+            V(lift_weight.shape, f32),
+            V((1, C), f32),
+            V(mix_weight.shape, bf16),
+            V((1, C), f32),
+            V((6, C * XL, YL), f32),
             V((C * XL, NZL * YL), bf16),
-            V((A, NZL * YL, L), bf16),
-            V((C * XL, L), bf16),
-            V((C * XL, L), bf16),
-            V((G, CB * XL, L), bf16),
-            V((G, CB * XL, L), bf16),
-            V((H, CB * KB, L), bf16),
-            V((H - 1, CB * KB, L), bf16),
-            V((CB * KB, L), bf16),
-            V((G, CB * KB, L), bf16),
+            V((A * NCH, NZL * YL, W), bf16),
+            V((NCH, C * XL, W), bf16),
+            V((NCH, C * XL, W), bf16),
+            V((NCH, G, CB * XL, W), bf16),
+            V((NCH, G, CB * XL, W), bf16),
+            V((NCH, H, CB * KB, W), bf16),
+            V((NCH, H - 1, CB * KB, W), bf16),
+            V((NCH, CB * KB, W), bf16),
+            V((NCH, G, CB * KB, W), bf16),
             V((KZ, C * KB, Q), f32),
             V((KZ, C * KB, Q), f32),
-            V((KB, OB, L), f32),
-            V((H, KB * OB, L), bf16),
-            V((H, KB * OB, L), bf16),
-            V((G, OB * XL, NZL * YL), bf16),
-            V((G, OB * XL, NZL * YL), bf16),
-            V(spectral_weight.shape, f32),
-            dma((6,)),
+            V((NCH, KB, OB, W), f32),
+            V((NCH, H, KB * OB, W), bf16),
+            V((NCH, H, KB * OB, W), bf16),
+            V((NZC, G, OB * XL, ZW), bf16),
+            V((NZC, G, OB * XL, ZW), bf16),
+            dma((10,)),
             dma((STEPS, 6)), dma((STEPS, 6)),
-            dma((1,)), dma((1,)),
-            dma((G - 1,)), dma((G - 1,)),
-            dma((H - 1,)), dma((H - 1,)),
-            dma((G - 1,)), dma((G - 1,)),
-            dma((H - 1,)), dma((H - 1,)),
-            dma((H,)), dma((H,)),
-            dma((G - 1,)), dma((G - 1,)),
+            dma((NCH,)), dma((NCH,)),
+            dma((NCH * (G - 1),)), dma((NCH * (G - 1),)),
+            dma((NCH * (H - 1),)), dma((NCH * (H - 1),)),
+            dma((NCH * (G - 1),)), dma((NCH * (G - 1),)),
+            dma((NCH * (H - 1),)), dma((NCH * (H - 1),)),
+            dma((NCH * H,)), dma((NCH * H,)),
+            dma((NZC * (G - 1),)), dma((NZC * (G - 1),)),
         ],
         compiler_params=pltpu.CompilerParams(collective_id=0, has_side_effects=True, vmem_limit_bytes=48 * 2**20),
     )(
-        lift_weight, lift_bias, mix_weight, output_bias[None, :],
-        jnp.asarray(np.cos(v), f32), jnp.asarray(np.sin(v), f32),
         fields, stiffness, ed, x1, x2, spectral_weight,
+        lift_weight, lift_bias[None, :], mix_weight, output_bias[None, :],
     )
 
 

time: 69.9 us -> 64.7 us (0.926)
  Pallas kernels: 59.6 us -> 55.9 us
  local copies, waits for them, and re-layouts: 9.81 us -> 8.42 us
    pallas_call x1, Pallas kernels: 59.6 us -> 55.9 us  [shards(): pl.pallas_call(functools.partial(layer_kernel, cfg), out_shape=jax.ShapeD...]
    unnamed x23 -> x19, local copies, waits for them, and re-layouts: 9.81 us -> 8.42 us
where the time goes in v3:
time: 64.7 us; the launch traced here: 64.3 us
  Pallas kernels  55.9 us (86%)
  local copies, waits for them, and re-layouts  8.42 us (13%)
    pallas_call x1, Pallas kernels, shards(): pl.pallas_call(functools.partial(layer_kernel, cfg), out_shape=jax.ShapeD...  55.9 us
    unnamed x19, local copies, waits for them, and re-layouts  8.42 us

profile of v3, /device:TPU:0, one launch (start us, length us, event | category | flops | bytes accessed | tf_op | source)
XLA Modules:
  0.0 64.3 jit_solution(11631234603856922946)
XLA Ops:
  0.0 0.0 copy-start
  0.0 1.1 %copy-done = f32[5,8,16,256]{3,2,1,0:T(8,128)S(1)} copy-done((f32[5,8,16,256]{3,2,1,0:T(8,128)S(1)}, f32[5,8,16,256]{3,2,1,0:T(8,128)}, u32[]{:S(2)}) %copy-start) | copy-done | bytes 655384
  1.1 0.0 copy-start.1
  1.1 1.0 %copy-done.1 = f32[4,2,128,128]{3,2,1,0:T(8,128)S(1)} copy-done((f32[4,2,128,128]{3,2,1,0:T(8,128)S(1)}, f32[4,2,128,128]{3,2,1,0:T(8,128)}, u32[]{:S(2)}) %copy-start.1) | copy-done | bytes 524312
  2.1 0.0 copy-start.2
  2.1 0.9 %copy-done.2 = bf16[256,512]{1,0:T(8,128)(2,1)S(1)} copy-done((bf16[256,512]{1,0:T(8,128)(2,1)S(1)}, bf16[256,512]{1,0:T(8,128)(2,1)}, u32[]{:S(2)}) %copy-start.2) | copy-done | bytes 262168
  3.1 0.0 copy-start.3
  3.1 0.9 %copy-done.3 = bf16[256,512]{1,0:T(8,128)(2,1)S(1)} copy-done((bf16[256,512]{1,0:T(8,128)(2,1)S(1)}, bf16[256,512]{1,0:T(8,128)(2,1)}, u32[]{:S(2)}) %copy-start.3) | copy-done | bytes 262168
  4.0 0.0 copy-start.4
  4.0 0.9 %copy-done.4 = f32[8,16,256]{2,1,0:T(8,128)S(1)} copy-done((f32[8,16,256]{2,1,0:T(8,128)S(1)}, f32[8,16,256]{2,1,0:T(8,128)}, u32[]{:S(2)}) %copy-start.4) | copy-done | bytes 131096
  4.9 0.0 copy-start.5
  4.9 0.7 %copy-done.5 = bf16[32,32]{1,0:T(8,128)(2,1)S(1)} copy-done((bf16[32,32]{1,0:T(8,128)(2,1)S(1)}, bf16[32,32]{1,0:T(8,128)(2,1)}, u32[]{:S(2)}) %copy-start.5) | copy-done | bytes 2072
  5.6 0.0 copy-start.6
  5.6 0.7 %copy-done.6 = f32[5,32]{1,0:T(8,128)S(1)} copy-done((f32[5,32]{1,0:T(8,128)S(1)}, f32[5,32]{1,0:T(8,128)}, u32[]{:S(2)}) %copy-start.6) | copy-done | bytes 664
  6.3 0.0 copy-start.7
  6.3 0.7 %copy-done.7 = f32[32]{0:T(128)S(1)} copy-done((f32[32]{0:T(128)S(1)}, f32[32]{0:T(128)}, u32[]{:S(2)}) %copy-start.7) | copy-done | bytes 152
  7.0 0.0 copy-start.8
  7.0 0.7 %copy-done.8 = f32[32]{0:T(128)S(1)} copy-done((f32[32]{0:T(128)S(1)}, f32[32]{0:T(128)}, u32[]{:S(2)}) %copy-start.8) | copy-done | bytes 152
  7.6 55.9 %shard_map.100 = bf16[8,32,8,128]{3,2,1,0:T(8,128)(2,1)S(1)} custom-call(f32[5,8,16,256]{3,2,1,0:T(8,128)S(1)} %copy-done, f32[8,16,256]{2,1,0:T(8,128)S(1)} %copy-done.4, f32[4,2,128,128]{3,2,1,0:T(8,128)S(1)} %copy-done.1, bf16[256,512]{1,0:T(8,128)(2,1)S(1)} %copy-done.3, bf16[256,512]{1,0:T(8,128)(2,1)S(1)} %copy-done.2, f32[4,8,32,8,128]{4,3,2,1,0:T(8,128)} %w_hbm.1, ...), custom_call_target="tpu_custom_call" | custom-call | tf_op jit(solution)/shard_map/pallas_call | solution.py:453
  63.5 0.8 %copy.12 = bf16[8,32,8,128]{3,2,1,0:T(8,128)(2,1)} copy(bf16[8,32,8,128]{3,2,1,0:T(8,128)(2,1)S(1)} %shard_map.100) | data formatting | bytes 1048576
Async XLA Ops:
  0.0 1.1 %copy-start = (f32[5,8,16,256]{3,2,1,0:T(8,128)S(1)}, f32[5,8,16,256]{3,2,1,0:T(8,128)}, u32[]{:S(2)}) copy-start(f32[5,8,16,256]{3,2,1,0:T(8,128)} %fields_hbm.1) | copy-start | bytes 1966084
  1.1 1.0 %copy-start.1 = (f32[4,2,128,128]{3,2,1,0:T(8,128)S(1)}, f32[4,2,128,128]{3,2,1,0:T(8,128)}, u32[]{:S(2)}) copy-start(f32[4,2,128,128]{3,2,1,0:T(8,128)} %constant.8.clone.ed_hbm) | copy-start | bytes 1572868
  2.1 0.9 %copy-start.2 = (bf16[256,512]{1,0:T(8,128)(2,1)S(1)}, bf16[256,512]{1,0:T(8,128)(2,1)}, u32[]{:S(2)}) copy-start(bf16[256,512]{1,0:T(8,128)(2,1)} %constant.7.clone.x2_hbm) | copy-start | bytes 786436
  3.1 0.9 %copy-start.3 = (bf16[256,512]{1,0:T(8,128)(2,1)S(1)}, bf16[256,512]{1,0:T(8,128)(2,1)}, u32[]{:S(2)}) copy-start(bf16[256,512]{1,0:T(8,128)(2,1)} %constant.6.clone.x1_hbm) | copy-start | bytes 786436
  4.0 0.9 %copy-start.4 = (f32[8,16,256]{2,1,0:T(8,128)S(1)}, f32[8,16,256]{2,1,0:T(8,128)}, u32[]{:S(2)}) copy-start(f32[8,16,256]{2,1,0:T(8,128)} %stiff_hbm.1) | copy-start | bytes 393220
  4.9 0.7 %copy-start.5 = (bf16[32,32]{1,0:T(8,128)(2,1)S(1)}, bf16[32,32]{1,0:T(8,128)(2,1)}, u32[]{:S(2)}) copy-start(bf16[32,32]{1,0:T(8,128)(2,1)} %mix_hbm.1) | copy-start | bytes 6148
  5.6 0.7 %copy-start.6 = (f32[5,32]{1,0:T(8,128)S(1)}, f32[5,32]{1,0:T(8,128)}, u32[]{:S(2)}) copy-start(f32[5,32]{1,0:T(8,128)} %lw_hbm.1) | copy-start | bytes 1924
  6.3 0.7 %copy-start.7 = (f32[32]{0:T(128)S(1)}, f32[32]{0:T(128)}, u32[]{:S(2)}) copy-start(f32[32]{0:T(128)} %param.13) | copy-start | bytes 388
  7.0 0.7 %copy-start.8 = (f32[32]{0:T(128)S(1)}, f32[32]{0:T(128)}, u32[]{:S(2)}) copy-start(f32[32]{0:T(128)} %param.16) | copy-start | bytes 388

commit v4 on v3

--- a/solution.py
+++ b/solution.py
@@ -13,7 +13,7 @@
 MX = 32
 MY = 64
 MZ = 8
-MODE_CHUNKS = 2
+MODE_CHUNKS = 4
 DEPTH_CHUNKS = 4
 
 
@@ -500,7 +500,7 @@
             dma((NCH * H,)), dma((NCH * H,)),
             dma((NZC * (G - 1),)), dma((NZC * (G - 1),)),
         ],
-        compiler_params=pltpu.CompilerParams(collective_id=0, has_side_effects=True, vmem_limit_bytes=48 * 2**20),
+        compiler_params=pltpu.CompilerParams(collective_id=0, has_side_effects=True, vmem_limit_bytes=67043328),
     )(
         fields, stiffness, ed, x1, x2, spectral_weight,
         lift_weight, lift_bias[None, :], mix_weight, output_bias[None, :],

time: 64.7 us -> 57.9 us (0.89)
  local copies, waits for them, and re-layouts: 8.42 us -> 1.87 us
    unnamed x19 -> x1, local copies, waits for them, and re-layouts: 8.42 us -> 1.87 us
where the time goes in v4:
time: 57.9 us; the launch traced here: 57.8 us
  Pallas kernels  55.9 us (97%)
  local copies, waits for them, and re-layouts  1.87 us (3%)
    pallas_call x1, Pallas kernels, shards(): pl.pallas_call(functools.partial(layer_kernel, cfg), out_shape=jax.ShapeD...  55.9 us
    unnamed x1, local copies, waits for them, and re-layouts  1.87 us

profile of v4, /device:TPU:0, one launch (start us, length us, event | category | flops | bytes accessed | tf_op | source)
XLA Modules:
  0.0 57.8 jit_solution(10822550723164642963)
XLA Ops:
  0.0 55.9 %shard_map.100 = bf16[8,32,8,128]{3,2,1,0:T(8,128)(2,1)} custom-call(f32[5,8,16,256]{3,2,1,0:T(8,128)} %fields_hbm.1, f32[8,16,256]{2,1,0:T(8,128)} %stiff_hbm.1, f32[4,2,128,128]{3,2,1,0:T(8,128)} %constant.8.clone.ed_hbm, bf16[256,512]{1,0:T(8,128)(2,1)} %constant.6.clone.x1_hbm, bf16[256,512]{1,0:T(8,128)(2,1)} %constant.7.clone.x2_hbm, ...), custom_call_target="tpu_custom_call" | custom-call | tf_op jit(solution)/shard_map/pallas_call | solution.py:453
  55.9 1.9 %copy.12 = bf16[8,32,8,128]{3,2,1,0:T(8,128)(2,1)} copy(bf16[8,32,8,128]{3,2,1,0:T(8,128)(2,1)} %shard_map.100) | data formatting | bytes 1048576
